TPU v7x, 32 devices: a whole 2x2x4 slice. The times are simulated.
32 devices in a mesh: seq: 8 (over y, x, core), head: 4 (over z).
Axes of the slice: x: 2, y: 2, z: 4, core: 2. Of those that a mesh axis runs over, the one named last changes fastest.
Arguments:
- tokens: bfloat16 [2048, 2048], P('seq'), may hold values from -6 to 6
- w_query: bfloat16 [2048, 2048], P(None, 'head'), may hold values from -0.125 to 0.125
- w_key: bfloat16 [2048, 2048], P(None, 'head'), may hold values from -0.125 to 0.125
- w_value: bfloat16 [2048, 2048], P(None, 'head'), may hold values from -0.125 to 0.125
- w_beta: bfloat16 [2048, 16], P(None, 'head'), may hold values from -0.125 to 0.125
- b_beta: float32 [16], P('head'), may hold values from -6 to 1
- d_out: bfloat16 [2048, 2048], P('seq', 'head'), may hold values from -6 to 6
Outputs:
- d_x: bfloat16 [2048, 2048], P('seq', 'head')
- grad_query: float32 [2048, 2048], P('seq', 'head')
- grad_key: float32 [2048, 2048], P('seq', 'head')
- grad_value: float32 [2048, 2048], P('seq', 'head')
- grad_wbeta: float32 [2048, 16], P('seq', 'head')
- grad_bbeta: float32 [16], P('head')
All inputs are finite; a program needn't handle non-finite values.
Results may differ from a plain program's by a relative error of at most 0.012.
Values may be sent and summed in bfloat16 or wider, within the bound.
A program may use at most 128 MiB of HBM per device.

v0:
```python
import functools

import jax
import jax.numpy as jnp
from jax import lax
from jax.experimental import pallas as pl
from jax.experimental.pallas import tpu as pltpu
from jax.sharding import PartitionSpec as P

epsilon = 1e-06
LANES = 128
MESH = pl.DeviceIdType.MESH
highest = lax.Precision.HIGHEST


def split(a):
    high = a.astype(jnp.bfloat16)
    return high, (a - high.astype(jnp.float32)).astype(jnp.bfloat16)


def only(a):
    return a.astype(jnp.bfloat16), None


def mm(a, b, dims=(1, 0)):
    numbers = (((dims[0],), (dims[1],)), ((), ()))
    dot = functools.partial(
        lax.dot_general, dimension_numbers=numbers, preferred_element_type=jnp.float32
    )
    total = dot(a[0], b[0])
    if b[1] is not None:
        total = total + dot(a[0], b[1])
    if a[1] is not None:
        total = total + dot(a[1], b[0])
    return total


def iotas(rows, cols):
    return (
        lax.broadcasted_iota(jnp.int32, (rows, cols), 0),
        lax.broadcasted_iota(jnp.int32, (rows, cols), 1),
    )


def invert_unit_lower(systems):
    size = systems[0].shape[0]
    base = min(size, LANES)
    row, col = iotas(base, base)
    eye = jnp.where(row == col, 1.0, 0.0).astype(jnp.float32)

    def step_mask(s):
        return (row // (2 * s) == col // (2 * s)) & (row % (2 * s) >= s) & (col % (2 * s) < s)

    count = size // base
    diagonals = [
        n[i * base : (i + 1) * base, i * base : (i + 1) * base] for n in systems for i in range(count)
    ]
    inverses = [eye - jnp.where(step_mask(1), n, 0.0) for n in diagonals]
    s = 2
    while s < base:
        mask = step_mask(s)
        parts = [split(x) for x in inverses]
        inner = [mm(split(jnp.where(mask, n, 0.0)), x) for n, x in zip(diagonals, parts)]
        outer = [mm(x, split(y)) for x, y in zip(parts, inner)]
        inverses = [x - y for x, y in zip(inverses, outer)]
        s *= 2
    grouped = [inverses[i * count : (i + 1) * count] for i in range(len(systems))]
    width = base
    while width < size:
        merged = []
        for n, blocks in zip(systems, grouped):
            joined = []
            for i in range(0, len(blocks), 2):
                first, second = blocks[i], blocks[i + 1]
                low = n[(i + 1) * width : (i + 2) * width, i * width : (i + 1) * width]
                corner = mm(split(second), split(mm(split(low), split(first))))
                joined.append(
                    jnp.concatenate(
                        [
                            jnp.concatenate([first, jnp.zeros_like(first)], 1),
                            jnp.concatenate([-corner, second], 1),
                        ],
                        0,
                    )
                )
            merged.append(joined)
        grouped = merged
        width *= 2
    return [g[0] for g in grouped]


def normalise(raw):
    scale = lax.rsqrt(jnp.sum(raw * raw, -1, keepdims=True) + epsilon)
    return raw * scale, scale


def meet(peers):
    barrier = pltpu.get_barrier_semaphore()
    for peer in peers:
        pl.semaphore_signal(barrier, inc=1, device_id=peer, device_id_type=MESH)
    pl.semaphore_wait(barrier, len(peers))


def exchange_summary_kernel(
    shards, heads, dim, x_ref, q_ref, k_ref, v_ref, z_ref, g_ref, map_ref, mid_ref, cols_ref, send, recv, here
):
    me = lax.axis_index("seq")
    rows = x_ref.shape[0]
    part = cols_ref.shape[1]
    peers = [lax.rem(me + r, shards) for r in range(1, shards)]
    meet([{"seq": p} for p in peers])

    def ends(p):
        return (
            x_ref.at[:, pl.ds(pl.multiple_of(p * part, part), part)],
            cols_ref.at[pl.ds(pl.multiple_of(me * rows, rows), rows), :],
        )

    copies = []
    for i, p in enumerate(peers):
        source, target = ends(p)
        copy = pltpu.make_async_remote_copy(
            src_ref=source,
            dst_ref=target,
            send_sem=send.at[i],
            recv_sem=recv.at[i],
            device_id={"seq": p},
            device_id_type=MESH,
        )
        copy.start()
        copies.append(copy)
    own = pltpu.make_async_copy(*ends(me), here)
    own.start()
    summary_kernel(heads, dim, q_ref, k_ref, v_ref, z_ref, g_ref, map_ref, mid_ref)
    own.wait()
    for copy in copies:
        copy.wait()


def finish_kernel(
    groups, grads_ref, cols_ref, wq_ref, wk_ref, wv_ref, wb_ref,
    dx_ref, gq_ref, gk_ref, gv_ref, tail_ref, sum_ref,
    held, piece, landed, send, recv, piece_send, piece_recv,
):
    me = lax.axis_index("seq")
    group = lax.axis_index("head")
    rows = grads_ref.shape[0]
    half = rows // 2
    width = gq_ref.shape[1]
    top, bottom = pl.ds(0, half), pl.ds(half, half)

    def other(o):
        index = me
        for bit in (1, 2, 4):
            if o & bit:
                index = index + bit - 2 * bit * ((me // bit) % 2)
        return index

    across, inner, outer = ({"seq": other(o)} for o in (1, 2, 4))
    others = [{"head": lax.rem(group + r, groups)} for r in range(1, groups)]
    meet([across, inner, outer] + others)

    def move(i, source, slot, part, device):
        return pltpu.make_async_remote_copy(
            src_ref=source.at[part, :],
            dst_ref=held.at[slot].at[part, :],
            send_sem=send.at[i],
            recv_sem=recv.at[i],
            device_id=device,
            device_id_type=MESH,
        )

    hops = [
        move(0, grads_ref, 1, pl.ds(0, rows), across),
        move(1, grads_ref, 2, top, inner),
        move(2, grads_ref, 2, bottom, inner),
        move(3, grads_ref, 4, bottom, outer),
        move(4, grads_ref, 4, top, outer),
        move(5, held.at[2], 6, top, outer),
        move(6, held.at[4], 6, bottom, inner),
        move(7, held.at[2], 3, top, across),
        move(8, held.at[2], 3, bottom, across),
        move(9, held.at[4], 5, top, across),
        move(10, held.at[4], 5, bottom, across),
        move(11, held.at[6], 7, top, across),
        move(12, held.at[6], 7, bottom, across),
    ]
    for i in (1, 3, 2, 4, 0):
        hops[i].start()

    def input_part(index):
        span = pl.ds(pl.multiple_of(index * width, width), width)
        total = lax.dot_general(
            grads_ref[:, 3 * width :], wb_ref[span, :], (((1,), (1,)), ((), ())),
            preferred_element_type=jnp.float32,
        )
        for i, w in enumerate((wq_ref, wk_ref, wv_ref)):
            total = total + lax.dot_general(
                grads_ref[:, i * width : (i + 1) * width], w[span, :], (((1,), (1,)), ((), ())),
                preferred_element_type=jnp.float32,
            )
        return total

    pieces = []
    for r in range(1, groups):
        piece[r] = input_part(lax.rem(group + r, groups)).astype(piece.dtype)
        copy = pltpu.make_async_remote_copy(
            src_ref=piece.at[r],
            dst_ref=landed.at[r],
            send_sem=piece_send.at[r],
            recv_sem=piece_recv.at[r],
            device_id=others[r - 1],
            device_id_type=MESH,
        )
        copy.start()
        pieces.append(copy)
    own = input_part(group)

    def add(o):
        block = grads_ref if o == 0 else held.at[o]
        span = pl.ds(pl.multiple_of(other(o) * rows, rows), rows)
        lhs = cols_ref[span, :].T
        for i, target in enumerate((gq_ref, gk_ref, gv_ref, tail_ref)):
            columns = slice(i * width, (i + 1) * width if i < 3 else None)
            value = jnp.dot(lhs, block[:, columns], preferred_element_type=jnp.float32)
            target[...] = value if o == 0 else target[...] + value
        total = jnp.sum(block[:, 3 * width :].astype(jnp.float32), 0, keepdims=True)
        sum_ref[...] = total if o == 0 else sum_ref[...] + total

    def arrive(i, *then):
        hops[i].wait_recv()
        for j in then:
            hops[j].start()

    add(0)
    arrive(0)
    add(1)
    arrive(1, 5, 7)
    arrive(3, 6, 10)
    arrive(2, 8)
    arrive(4, 9)
    add(2)
    add(4)
    arrive(7)
    arrive(8)
    add(3)
    arrive(9)
    arrive(10)
    add(5)
    for r, copy in enumerate(pieces, 1):
        copy.wait()
        own = own + landed[r].astype(jnp.float32)
    dx_ref[...] = own.astype(dx_ref.dtype)
    arrive(5, 11)
    arrive(6, 12)
    add(6)
    arrive(11)
    arrive(12)
    add(7)
    for hop in hops:
        hop.wait_send()


def place_kernel(count, *refs):
    sems = refs[-1]
    copies = [pltpu.make_async_copy(refs[i], refs[count + i], sems.at[i]) for i in range(count)]
    for copy in copies:
        copy.start()
    for copy in copies:
        copy.wait()


def place(arrays):
    count = len(arrays)
    return pl.pallas_call(
        functools.partial(place_kernel, count),
        out_shape=tuple(jax.ShapeDtypeStruct(a.shape, a.dtype) for a in arrays),
        in_specs=[pl.BlockSpec(memory_space=pltpu.VMEM)] * count,
        out_specs=(pl.BlockSpec(memory_space=pltpu.HBM),) * count,
        scratch_shapes=[pltpu.SemaphoreType.DMA((count,))],
        name="place",
    )(*arrays)


def summary_kernel(heads, dim, q_ref, k_ref, v_ref, z_ref, g_ref, map_ref, mid_ref):
    count = q_ref.shape[0]
    row, col = iotas(count, count)
    strict, inclusive = row > col, row >= col
    every = range(heads)
    cols = [slice(h * dim, (h + 1) * dim) for h in every]
    beta_all = 2.0 * jax.nn.sigmoid(z_ref[...])
    beta = [beta_all[:, h : h + 1] for h in every]
    qn = [normalise(q_ref[:, c])[0] for c in cols]
    kn = [normalise(k_ref[:, c])[0] for c in cols]
    ks = [split(x) for x in kn]
    qs = [split(x) for x in qn]
    gs = [(g_ref[:, c], None) for c in cols]
    gram = [jnp.where(strict, mm(x, x, (1, 1)), 0.0) for x in ks]
    inverse = [split(t) for t in invert_unit_lower([b * n for b, n in zip(beta, gram)])]
    gram = [split(n) for n in gram]
    scores = [split(jnp.where(inclusive, mm(a, b, (1, 1)), 0.0)) for a, b in zip(qs, ks)]
    back = [mm(p, g, (0, 0)) for p, g in zip(scores, gs)]
    forth_in = [jnp.concatenate([v_ref[:, c], k], 1) for c, k in zip(cols, kn)]
    forth = [split(mm(t, split(b * x))) for t, b, x in zip(inverse, beta, forth_in)]
    plain = [x - mm(n, f) for x, n, f in zip(forth_in, gram, forth)]
    adjoint = [
        mm(t, split(jnp.concatenate([p, k], 1)), (0, 0)) for t, p, k in zip(inverse, back, kn)
    ]
    ends = [mm(f, k, (0, 0)) for f, k in zip(forth, ks)]
    tails = [mm(split(a), split(b * k), (0, 0)) for a, b, k in zip(adjoint, beta, kn)]
    direct = [mm(g, q, (0, 0)) for g, q in zip(gs, qs)]
    for h in every:
        map_ref[h, 0] = ends[h][dim:].astype(map_ref.dtype)
        map_ref[h, 1] = ends[h][:dim].astype(map_ref.dtype)
        map_ref[heads + h, 0] = tails[h][dim:].astype(map_ref.dtype)
        map_ref[heads + h, 1] = (direct[h] - tails[h][:dim]).astype(map_ref.dtype)
        mid_ref[h, :, : 2 * dim] = plain[h]
        mid_ref[h, :, 2 * dim :] = adjoint[h]


def gradient_kernel(
    heads, dim, q_ref, k_ref, z_ref, g_ref, mid_ref, state_ref, out_ref
):
    count = q_ref.shape[0]
    row, col = iotas(count, count)
    strict, inclusive = row > col, row >= col
    beta_all = 2.0 * jax.nn.sigmoid(z_ref[...])
    width = heads * dim
    every = range(heads)
    cols = [slice(h * dim, (h + 1) * dim) for h in every]
    beta = [beta_all[:, h : h + 1] for h in every]
    qp = [normalise(q_ref[:, c]) for c in cols]
    kp = [normalise(k_ref[:, c]) for c in cols]
    ks = [split(x[0]) for x in kp]
    qs = [split(x[0]) for x in qp]
    gs = [(g_ref[:, c], None) for c in cols]
    ss = [(state_ref[h], None) for h in every]
    ds = [(state_ref[heads + h], None) for h in every]
    plain = [
        mid_ref[h, :, :dim] - mm(split(mid_ref[h, :, dim : 2 * dim]), ss[h], (1, 1)) for h in every
    ]
    dx = [
        mid_ref[h, :, 2 * dim : 3 * dim] + mm(split(mid_ref[h, :, 3 * dim :]), ds[h], (1, 1))
        for h in every
    ]
    us = [split(b * x) for b, x in zip(beta, plain)]
    dv = [b * x for b, x in zip(beta, dx)]
    dvs = [split(x) for x in dv]
    inner = [split(jnp.where(inclusive, mm(g, u, (1, 1)), 0.0)) for g, u in zip(gs, us)]
    pair = [jnp.where(strict, mm(d, u, (1, 1)), 0.0) for d, u in zip(dvs, us)]
    both = [split(e + e.T) for e in pair]
    dqn = [mm(g, s) + mm(i, k) for g, s, i, k in zip(gs, ss, inner, ks)]
    dkn = [
        mm(i, q, (0, 0)) + mm(u, d) - mm(x, s) - mm(e, k)
        for i, q, u, d, x, s, e, k in zip(inner, qs, us, ds, dvs, ss, both, ks)
    ]

    def through(grad, pair):
        unit, scale = pair
        return scale * (grad - unit * jnp.sum(unit * grad, -1, keepdims=True))

    lane = lax.broadcasted_iota(jnp.int32, (count, LANES), 1)
    last = jnp.zeros((count, LANES), jnp.float32)
    for h in every:
        out_ref[:, cols[h]] = through(dqn[h], qp[h]).astype(jnp.bfloat16)
        out_ref[:, width + h * dim : width + (h + 1) * dim] = through(dkn[h], kp[h]).astype(
            jnp.bfloat16
        )
        out_ref[:, 2 * width + h * dim : 2 * width + (h + 1) * dim] = dv[h].astype(jnp.bfloat16)
        dz = jnp.sum(dx[h] * plain[h], -1, keepdims=True) * beta[h] * (1.0 - 0.5 * beta[h])
        high, low = split(dz)
        last = jnp.where(lane == h, high.astype(jnp.float32), last)
        last = jnp.where(lane == heads + h, low.astype(jnp.float32), last)
    out_ref[:, 3 * width :] = last.astype(jnp.bfloat16)


def gathered_states(maps, heads):
    count = lax.axis_size("seq")
    place = lax.axis_index("seq")
    gathered = lax.all_gather(maps, "seq").astype(jnp.float32)

    def walk(steps, pick, rows):
        def one(lap, state):
            pair = lax.dynamic_index_in_dim(gathered, pick(lap), 0, False)[rows]
            moved = jnp.einsum("hij,hjk->hik", state, pair[:, 0], precision=highest)
            return state - moved + pair[:, 1]

        return lax.fori_loop(0, steps, one, jnp.zeros((heads,) + maps.shape[2:], jnp.float32))

    first = walk(place, lambda lap: lap, slice(0, heads))
    second = walk(count - 1 - place, lambda lap: count - 1 - lap, slice(heads, None))
    return jnp.concatenate([first, second]).astype(maps.dtype)


def states_kernel(count, heads, map_ref, out_ref, inbox, outbox, send, recv, send_back, recv_back):
    me = lax.axis_index("seq")
    barrier = pltpu.get_barrier_semaphore()
    for r in range(1, count):
        pl.semaphore_signal(
            barrier, inc=1, device_id={"seq": lax.rem(me + r, count)}, device_id_type=MESH
        )
    pl.semaphore_wait(barrier, count - 1)
    copies = []
    for r in range(1, count):
        peer = lax.rem(me + r, count)
        copy = pltpu.make_async_remote_copy(
            src_ref=map_ref.at[peer],
            dst_ref=inbox.at[r],
            send_sem=send.at[r],
            recv_sem=recv.at[r],
            device_id={"seq": peer},
            device_id_type=MESH,
        )
        copy.start()
        copies.append(copy)
    inbox[0] = map_ref[me]
    for copy in copies:
        copy.wait()
    backward = me // heads
    state = jnp.zeros(inbox.shape[2:], jnp.float32)

    def back(p):
        source = p + backward * (count - 1 - 2 * p)
        return source, pltpu.make_async_remote_copy(
            src_ref=outbox.at[p],
            dst_ref=out_ref.at[me],
            send_sem=send_back.at[p],
            recv_sem=recv_back.at[me],
            device_id={"seq": source},
            device_id_type=MESH,
        )

    for p in range(count):
        source, copy = back(p)
        outbox[p] = state.astype(outbox.dtype)

        @pl.when(source != me)
        def _():
            copy.start()

        @pl.when(source == me)
        def _():
            out_ref[me] = outbox[p]

        if p + 1 < count:
            slot = lax.rem(me - source + count, count)
            state = state - mm(split(state), (inbox[slot, 0], None)) + inbox[slot, 1].astype(
                jnp.float32
            )
    for p in range(count):
        source, copy = back(p)

        @pl.when(source != me)
        def _():
            copy.wait_send()

    for r in range(1, count):
        unit = lax.rem(me + r, count)
        pltpu.make_async_remote_copy(
            src_ref=outbox.at[r],
            dst_ref=out_ref.at[unit],
            send_sem=send_back.at[r],
            recv_sem=recv_back.at[unit],
            device_id={"seq": unit},
            device_id_type=MESH,
        ).wait_recv()


def boundary_states(maps, heads):
    count = lax.axis_size("seq")
    units, _, dim, _ = maps.shape
    if units != count:
        return gathered_states(maps, heads)
    vmem = pl.BlockSpec(memory_space=pltpu.VMEM)
    return pl.pallas_call(
        functools.partial(states_kernel, count, heads),
        out_shape=jax.ShapeDtypeStruct((units, dim, dim), maps.dtype),
        in_specs=[vmem],
        out_specs=vmem,
        scratch_shapes=[
            pltpu.VMEM(maps.shape, maps.dtype),
            pltpu.VMEM((count, dim, dim), maps.dtype),
            pltpu.SemaphoreType.DMA((count,)),
            pltpu.SemaphoreType.DMA((count,)),
            pltpu.SemaphoreType.DMA((count,)),
            pltpu.SemaphoreType.DMA((count,)),
        ],
        compiler_params=pltpu.CompilerParams(collective_id=0, has_side_effects=True),
        name="states",
    )(maps)


def per_device(tokens, w_query, w_key, w_value, w_beta, b_beta, d_out):
    token_count = tokens.shape[0]
    heads = w_beta.shape[1]
    width = w_query.shape[1]
    dim = width // heads
    f32 = jnp.float32
    q = jnp.dot(tokens, w_query, preferred_element_type=f32)
    k = jnp.dot(tokens, w_key, preferred_element_type=f32)
    v = jnp.dot(tokens, w_value, preferred_element_type=f32)
    w_last = jnp.pad(w_beta, ((0, 0), (0, LANES - heads)))
    z = jnp.dot(tokens, w_last, preferred_element_type=f32) + jnp.pad(b_beta, (0, LANES - heads))
    limit = 60 * 1024 * 1024
    params = pltpu.CompilerParams(vmem_limit_bytes=limit)
    shards, groups = lax.axis_size("seq"), lax.axis_size("head")
    columns_part = tokens.shape[1] // shards
    vmem = pl.BlockSpec(memory_space=pltpu.VMEM)
    routed = shards == 8 and columns_part % LANES == 0
    summary_shapes = (
        jax.ShapeDtypeStruct((2 * heads, 2, dim, dim), jnp.bfloat16),
        jax.ShapeDtypeStruct((heads, token_count, 4 * dim), f32),
    )
    if routed:
        maps, mid, columns = pl.pallas_call(
            functools.partial(exchange_summary_kernel, shards, heads, dim),
            out_shape=summary_shapes
            + (jax.ShapeDtypeStruct((token_count * shards, columns_part), tokens.dtype),),
            in_specs=[vmem] * 6,
            out_specs=(vmem,) * 3,
            scratch_shapes=[
                pltpu.SemaphoreType.DMA((shards - 1,)),
                pltpu.SemaphoreType.DMA((shards - 1,)),
                pltpu.SemaphoreType.DMA,
            ],
            compiler_params=pltpu.CompilerParams(
                vmem_limit_bytes=limit, collective_id=1, has_side_effects=True
            ),
            name="summary",
        )(tokens, q, k, v, z, d_out)
    else:
        columns = lax.all_to_all(tokens, "seq", split_axis=1, concat_axis=0, tiled=True)
        maps, mid = pl.pallas_call(
            functools.partial(summary_kernel, heads, dim),
            out_shape=summary_shapes,
            compiler_params=params,
            name="summary",
        )(q, k, v, z, d_out)
    states = boundary_states(maps, heads)
    grads = pl.pallas_call(
        functools.partial(gradient_kernel, heads, dim),
        out_shape=jax.ShapeDtypeStruct((token_count, 3 * width + LANES), jnp.bfloat16),
        compiler_params=params,
        name="gradient",
    )(q, k, z, d_out, mid, states)
    weights = (w_query, w_key, w_value)
    if routed:
        square = jax.ShapeDtypeStruct((columns_part, width), f32)
        d_x, grad_q, grad_k, grad_v, tail, sums = pl.pallas_call(
            functools.partial(finish_kernel, groups),
            out_shape=(
                jax.ShapeDtypeStruct((token_count, tokens.shape[1] // groups), tokens.dtype),
                square,
                square,
                square,
                jax.ShapeDtypeStruct((columns_part, LANES), f32),
                jax.ShapeDtypeStruct((1, LANES), f32),
            ),
            in_specs=[vmem] * 6,
            out_specs=(vmem,) * 6,
            scratch_shapes=[
                pltpu.VMEM((8,) + grads.shape, grads.dtype),
                pltpu.VMEM((groups, token_count, width), grads.dtype),
                pltpu.VMEM((groups, token_count, width), grads.dtype),
                pltpu.SemaphoreType.DMA((13,)),
                pltpu.SemaphoreType.DMA((13,)),
                pltpu.SemaphoreType.DMA((groups,)),
                pltpu.SemaphoreType.DMA((groups,)),
            ],
            compiler_params=pltpu.CompilerParams(
                vmem_limit_bytes=limit, collective_id=2, has_side_effects=True
            ),
            name="finish",
        )(grads, columns, *weights, w_last)
        bias = sums[0, :heads] + sums[0, heads : 2 * heads]
        d_x, grad_q, grad_k, grad_v = place((d_x, grad_q, grad_k, grad_v))
        return (d_x, grad_q, grad_k, grad_v, tail[:, :heads], bias)
    whole = lax.all_gather(grads, "seq", axis=0, tiled=True)
    partial = jnp.dot(grads[:, 3 * width : 3 * width + heads], w_beta.T, preferred_element_type=f32)
    for i, w in enumerate(weights):
        partial = partial + jnp.dot(
            grads[:, i * width : (i + 1) * width], w.T, preferred_element_type=f32
        )
    d_x = lax.psum_scatter(
        partial.astype(jnp.bfloat16), "head", scatter_dimension=1, tiled=True
    )

    def weight_grad(block):
        return lax.dot_general(
            columns, block, (((0,), (0,)), ((), ())), preferred_element_type=f32
        )

    found = [weight_grad(whole[:, i * width : (i + 1) * width]) for i in range(3)]
    tail = whole[:, 3 * width :]
    grad_wbeta = weight_grad(tail)[:, :heads]
    sums = jnp.sum(tail.astype(f32), 0)
    return (d_x, *found, grad_wbeta, sums[:heads] + sums[heads : 2 * heads])


def solution(mesh):
    in_specs = (
        P("seq", None),
        P(None, "head"),
        P(None, "head"),
        P(None, "head"),
        P(None, "head"),
        P("head"),
        P("seq", "head"),
    )
    out_specs = (
        P("seq", "head"),
        P("seq", "head"),
        P("seq", "head"),
        P("seq", "head"),
        P("seq", "head"),
        P("head"),
    )
    return jax.shard_map(
        per_device, mesh=mesh, in_specs=in_specs, out_specs=out_specs, check_vma=False
    )
```

profile of v0, /device:TPU:0, one launch (start us, length us, event | category | flops | bytes accessed | tf_op | source)
XLA Modules:
  0.0 98.3 jit_solution(14033704142645046606)
XLA Ops:
  0.6 0.0 copy-start
  0.6 0.7 pad.9
  1.4 1.0 %copy.13 = bf16[2048,4]{1,0:T(8,128)(2,1)S(1)} copy(bf16[2048,4]{0,1:T(4,128)(2,1)} %param.11) | data formatting | bytes 32768 | tf_op args[4]
  2.4 0.0 copy-start.1
  2.4 2.5 %fusion.z_ref = f32[256,128]{1,0:T(8,128)} fusion(bf16[256,2048]{1,0:T(8,128)(2,1)} %x_ref.1, f32[128]{0:T(128)S(1)} %pad.9, bf16[2048,4]{1,0:T(8,128)(2,1)S(1)} %copy.13), kind=kOutput, calls=%fused_computation.1 | convolution fusion | flops 134250496 | bytes 1196544 | tf_op jit(solution)/shard_map/dot_general | solution.py:503
  4.9 0.9 pad.8.wb_ref
  5.8 0.0 copy-done
  5.8 0.0 copy-done.1
  5.8 0.0 copy-start.2
  5.8 1.5 %fusion.3.q_ref = f32[256,512]{1,0:T(8,128)} fusion(bf16[256,2048]{1,0:T(8,128)(2,1)S(1)} %copy-done, bf16[2048,512]{1,0:T(8,128)(2,1)S(1)} %copy-done.1), kind=kOutput, calls=%fused_computation.5 | convolution fusion | flops 536870912 | bytes 3670016 | tf_op jit(solution)/shard_map/dot_general | solution.py:499
  7.3 0.1 copy-done.2
  7.4 0.0 copy-start.3
  7.4 1.5 %fusion.4.k_ref = f32[256,512]{1,0:T(8,128)} fusion(bf16[256,2048]{1,0:T(8,128)(2,1)S(1)} %copy-done, bf16[2048,512]{1,0:T(8,128)(2,1)S(1)} %copy-done.2), kind=kOutput, calls=%fused_computation.6 | convolution fusion | flops 536870912 | bytes 3670016 | tf_op jit(solution)/shard_map/dot_general | solution.py:500
  8.9 0.1 copy-done.3
  9.0 1.5 %fusion.5.v_ref = f32[256,512]{1,0:T(8,128)} fusion(bf16[256,2048]{1,0:T(8,128)(2,1)S(1)} %copy-done, bf16[2048,512]{1,0:T(8,128)(2,1)S(1)} %copy-done.3), kind=kOutput, calls=%fused_computation.7 | convolution fusion | flops 536870912 | bytes 3670016 | tf_op jit(solution)/shard_map/dot_general | solution.py:501
  10.5 19.4 %summary.1 = (bf16[8,2,128,128]{3,2,1,0:T(8,128)(2,1)}, f32[4,256,512]{2,1,0:T(8,128)}, bf16[2048,256]{1,0:T(8,128)(2,1)}) custom-call(bf16[256,2048]{1,0:T(8,128)(2,1)} %x_ref.1, f32[256,512]{1,0:T(8,128)} %fusion.3.q_ref, f32[256,512]{1,0:T(8,128)} %fusion.4.k_ref, f32[256,512]{1,0:T(8,128)} %fusion.5.v_ref, f32[256,128]{1,0:T(8,128)} %fusion.z_ref, ...), custom_call_target="tpu_custom_call" | custom-call | tf_op jit(solution)/shard_map/summary/pallas_call | solution.py:515
  29.9 18.1 %states.1.state_ref = bf16[8,128,128]{2,1,0:T(8,128)(2,1)} custom-call(bf16[8,2,128,128]{3,2,1,0:T(8,128)(2,1)} %get-tuple-element.20.map_ref), custom_call_target="tpu_custom_call" | custom-call | tf_op jit(solution)/shard_map/states/pallas_call | solution.py:475
  48.0 6.1 %gradient.1.grads_ref = bf16[256,1664]{1,0:T(8,128)(2,1)} custom-call(f32[256,512]{1,0:T(8,128)} %fusion.3.q_ref, f32[256,512]{1,0:T(8,128)} %fusion.4.k_ref, f32[256,128]{1,0:T(8,128)} %fusion.z_ref, bf16[256,512]{1,0:T(8,128)(2,1)} %g_ref.3, f32[4,256,512]{2,1,0:T(8,128)} %get-tuple-element.19.mid_ref, bf16[8,128,128]{2,1,0:T(8,128)(2,1)} %states.1.state_ref), custom_call_target="tpu_custom_call" | custom-call | tf_op jit(solution)/shard_map/gradient/pallas_call | solution.py:540
  54.1 38.7 %finish.1 = (bf16[256,512]{1,0:T(8,128)(2,1)}, f32[256,512]{1,0:T(8,128)}, f32[256,512]{1,0:T(8,128)}, f32[256,512]{1,0:T(8,128)}, f32[256,128]{1,0:T(8,128)}, /*index=5*/f32[1,128]{1,0:T(1,128)}) custom-call(bf16[256,1664]{1,0:T(8,128)(2,1)} %gradient.1.grads_ref, bf16[2048,256]{1,0:T(8,128)(2,1)} %get-tuple-element.21.cols_ref, bf16[2048,512]{1,0:T(8,128)(2,1)} %wq_ref.1, ...), custom_call_target="tpu_custom_call" | custom-call | tf_op jit(solution)/shard_map/finish/pallas_call | solution.py:549
  92.8 2.7 %place.1 = (bf16[256,512]{1,0:T(8,128)(2,1)}, f32[256,512]{1,0:T(8,128)}, f32[256,512]{1,0:T(8,128)}, f32[256,512]{1,0:T(8,128)}) custom-call(bf16[256,512]{1,0:T(8,128)(2,1)} %get-tuple-element.22.refs_0_, f32[256,512]{1,0:T(8,128)} %get-tuple-element.23.refs_1_, f32[256,512]{1,0:T(8,128)} %get-tuple-element.24.refs_2_, f32[256,512]{1,0:T(8,128)} %get-tuple-element.25.refs_3_), custom_call_target="tpu_custom_call" | custom-call | tf_op jit(solution)/shard_map/place/pallas_call | solution.py:275
  95.5 1.3 %add_bitcast_fusion = f32[4]{0:T(128)} fusion(f32[1,128]{1,0:T(1,128)} %get-tuple-element.31), kind=kLoop, calls=%fused_computation.2 | loop fusion | flops 4 | bytes 48 | tf_op jit(solution)/shard_map/add | solution.py:575
  96.7 1.6 %copy.15 = f32[256,4]{0,1:T(4,128)} copy(f32[256,4]{1,0:T(8,128)} %bitcast.12) | data formatting | bytes 8192
Async XLA Ops:
  0.6 5.1 %copy-start = (bf16[256,2048]{1,0:T(8,128)(2,1)S(1)}, bf16[256,2048]{1,0:T(8,128)(2,1)}, u32[]{:S(2)}) copy-start(bf16[256,2048]{1,0:T(8,128)(2,1)} %x_ref.1) | copy-start | bytes 3145732
  2.4 3.4 %copy-start.1 = (bf16[2048,512]{1,0:T(8,128)(2,1)S(1)}, bf16[2048,512]{1,0:T(8,128)(2,1)}, u32[]{:S(2)}) copy-start(bf16[2048,512]{1,0:T(8,128)(2,1)} %wq_ref.1) | copy-start | bytes 6291460
  5.8 1.6 %copy-start.2 = (bf16[2048,512]{1,0:T(8,128)(2,1)S(1)}, bf16[2048,512]{1,0:T(8,128)(2,1)}, u32[]{:S(2)}) copy-start(bf16[2048,512]{1,0:T(8,128)(2,1)} %wk_ref.1) | copy-start | bytes 6291460
  7.4 1.6 %copy-start.3 = (bf16[2048,512]{1,0:T(8,128)(2,1)S(1)}, bf16[2048,512]{1,0:T(8,128)(2,1)}, u32[]{:S(2)}) copy-start(bf16[2048,512]{1,0:T(8,128)(2,1)} %wv_ref.1) | copy-start | bytes 6291460
where the time goes:
time: 99.1 us; the launch traced here: 98.3 us
  Pallas kernels  85 us (86%)
  matrix products  6.95 us (7%)
  local copies, waits for them, and re-layouts  4.43 us (4%)
  other arithmetic  1.26 us (1%)
    pallas_call x1, Pallas kernels, per_device(): pl.pallas_call(functools.partial(finish_kernel, groups), out_shape=(jax.S...  38.7 us
    pallas_call x1, Pallas kernels, per_device(): pl.pallas_call(functools.partial(exchange_summary_kernel, shards, heads,...  19.4 us
    pallas_call x1, Pallas kernels, boundary_states(): pl.pallas_call(functools.partial(states_kernel, count, heads), out_shape=...  18.1 us
    pallas_call x1, Pallas kernels, per_device(): pl.pallas_call(functools.partial(gradient_kernel, heads, dim), out_shape=...  6.09 us
    unnamed x10, local copies, waits for them, and re-layouts  2.8 us
    pallas_call x1, Pallas kernels, place(): pl.pallas_call(functools.partial(place_kernel, count), out_shape=tuple((j...  2.7 us
    dot_general x1, matrix products, per_device(): jnp.dot(tokens, w_last, preferred_element_type=f32)  2.46 us

commit v1 on v0

v1 whole, which is shorter than its diff:
```python
import functools

import jax
import jax.numpy as jnp
from jax import lax
from jax.experimental import pallas as pl
from jax.experimental.pallas import tpu as pltpu
from jax.sharding import PartitionSpec as P

epsilon = 1e-06
LANES = 128
MESH = pl.DeviceIdType.MESH
highest = lax.Precision.HIGHEST


def split(a):
    high = a.astype(jnp.bfloat16)
    return high, (a - high.astype(jnp.float32)).astype(jnp.bfloat16)


def only(a):
    return a.astype(jnp.bfloat16), None


def mm(a, b, dims=(1, 0)):
    numbers = (((dims[0],), (dims[1],)), ((), ()))
    dot = functools.partial(
        lax.dot_general, dimension_numbers=numbers, preferred_element_type=jnp.float32
    )
    total = dot(a[0], b[0])
    if b[1] is not None:
        total = total + dot(a[0], b[1])
    if a[1] is not None:
        total = total + dot(a[1], b[0])
    return total


def iotas(rows, cols):
    return (
        lax.broadcasted_iota(jnp.int32, (rows, cols), 0),
        lax.broadcasted_iota(jnp.int32, (rows, cols), 1),
    )


def invert_unit_lower(systems):
    size = systems[0].shape[0]
    base = min(size, LANES)
    row, col = iotas(base, base)
    eye = jnp.where(row == col, 1.0, 0.0).astype(jnp.float32)

    def step_mask(s):
        return (row // (2 * s) == col // (2 * s)) & (row % (2 * s) >= s) & (col % (2 * s) < s)

    count = size // base
    diagonals = [
        n[i * base : (i + 1) * base, i * base : (i + 1) * base] for n in systems for i in range(count)
    ]
    inverses = [eye - jnp.where(step_mask(1), n, 0.0) for n in diagonals]
    s = 2
    while s < base:
        mask = step_mask(s)
        parts = [split(x) for x in inverses]
        inner = [mm(split(jnp.where(mask, n, 0.0)), x) for n, x in zip(diagonals, parts)]
        outer = [mm(x, split(y)) for x, y in zip(parts, inner)]
        inverses = [x - y for x, y in zip(inverses, outer)]
        s *= 2
    grouped = [inverses[i * count : (i + 1) * count] for i in range(len(systems))]
    width = base
    while width < size:
        merged = []
        for n, blocks in zip(systems, grouped):
            joined = []
            for i in range(0, len(blocks), 2):
                first, second = blocks[i], blocks[i + 1]
                low = n[(i + 1) * width : (i + 2) * width, i * width : (i + 1) * width]
                corner = mm(split(second), split(mm(split(low), split(first))))
                joined.append(
                    jnp.concatenate(
                        [
                            jnp.concatenate([first, jnp.zeros_like(first)], 1),
                            jnp.concatenate([-corner, second], 1),
                        ],
                        0,
                    )
                )
            merged.append(joined)
        grouped = merged
        width *= 2
    return [g[0] for g in grouped]


def normalise(raw):
    scale = lax.rsqrt(jnp.sum(raw * raw, -1, keepdims=True) + epsilon)
    return raw * scale, scale


def dot(a, b, dims=(1, 0)):
    return lax.dot_general(
        a, b, (((dims[0],), (dims[1],)), ((), ())), preferred_element_type=jnp.float32
    )


def summarise(heads, dim, q_ref, k_ref, v_ref, z_ref, g_ref, put_map):
    count = q_ref.shape[0]
    row, col = iotas(count, count)
    strict, inclusive = row > col, row >= col
    every = range(heads)
    cols = [slice(h * dim, (h + 1) * dim) for h in every]
    beta_all = 2.0 * jax.nn.sigmoid(z_ref[...])
    beta = [beta_all[:, h : h + 1] for h in every]
    qn = [normalise(q_ref[:, c])[0] for c in cols]
    kn = [normalise(k_ref[:, c])[0] for c in cols]
    ks = [split(x) for x in kn]
    qs = [split(x) for x in qn]
    gs = [(g_ref[:, c], None) for c in cols]
    gram = [jnp.where(strict, mm(x, x, (1, 1)), 0.0) for x in ks]
    inverse = [split(t) for t in invert_unit_lower([b * n for b, n in zip(beta, gram)])]
    gram = [split(n) for n in gram]
    scores = [split(jnp.where(inclusive, mm(a, b, (1, 1)), 0.0)) for a, b in zip(qs, ks)]
    back = [mm(p, g, (0, 0)) for p, g in zip(scores, gs)]
    forth_in = [jnp.concatenate([v_ref[:, c], k], 1) for c, k in zip(cols, kn)]
    forth = [split(mm(t, split(b * x))) for t, b, x in zip(inverse, beta, forth_in)]
    adjoint = [
        mm(t, split(jnp.concatenate([p, k], 1)), (0, 0)) for t, p, k in zip(inverse, back, kn)
    ]
    ends = [mm(f, k, (0, 0)) for f, k in zip(forth, ks)]
    tails = [mm(split(a), split(b * k), (0, 0)) for a, b, k in zip(adjoint, beta, kn)]
    direct = [mm(g, q, (0, 0)) for g, q in zip(gs, qs)]
    for h in every:
        put_map(h, ends[h][dim:], ends[h][:dim])
        put_map(heads + h, tails[h][dim:], direct[h] - tails[h][:dim])

    def put_mid(mid_ref):
        for h in every:
            mid_ref[h, :, : 2 * dim] = forth_in[h] - mm(gram[h], forth[h])
            mid_ref[h, :, 2 * dim :] = adjoint[h]

    return put_mid


def summary_kernel(heads, dim, q_ref, k_ref, v_ref, z_ref, g_ref, map_ref, mid_ref):
    def put_map(unit, factor, offset):
        map_ref[unit, 0] = factor.astype(map_ref.dtype)
        map_ref[unit, 1] = offset.astype(map_ref.dtype)

    summarise(heads, dim, q_ref, k_ref, v_ref, z_ref, g_ref, put_map)(mid_ref)


def gradients(heads, dim, every, q_ref, k_ref, z_ref, g_ref, mid_ref, state, put):
    count = q_ref.shape[0]
    row, col = iotas(count, count)
    strict, inclusive = row > col, row >= col
    beta_all = 2.0 * jax.nn.sigmoid(z_ref[...])
    cols = [slice(h * dim, (h + 1) * dim) for h in every]
    beta = [beta_all[:, h : h + 1] for h in every]
    qp = [normalise(q_ref[:, c]) for c in cols]
    kp = [normalise(k_ref[:, c]) for c in cols]
    ks = [split(x[0]) for x in kp]
    qs = [split(x[0]) for x in qp]
    gs = [(g_ref[:, c], None) for c in cols]
    ss = [(state(h), None) for h in every]
    ds = [(state(heads + h), None) for h in every]
    plain = [
        mid_ref[h, :, :dim] - mm(split(mid_ref[h, :, dim : 2 * dim]), s, (1, 1))
        for h, s in zip(every, ss)
    ]
    dx = [
        mid_ref[h, :, 2 * dim : 3 * dim] + mm(split(mid_ref[h, :, 3 * dim :]), d, (1, 1))
        for h, d in zip(every, ds)
    ]
    us = [split(b * x) for b, x in zip(beta, plain)]
    dv = [b * x for b, x in zip(beta, dx)]
    dvs = [split(x) for x in dv]
    inner = [split(jnp.where(inclusive, mm(g, u, (1, 1)), 0.0)) for g, u in zip(gs, us)]
    pair = [jnp.where(strict, mm(d, u, (1, 1)), 0.0) for d, u in zip(dvs, us)]
    both = [split(e + e.T) for e in pair]
    dqn = [mm(g, s) + mm(i, k) for g, s, i, k in zip(gs, ss, inner, ks)]
    dkn = [
        mm(i, q, (0, 0)) + mm(u, d) - mm(x, s) - mm(e, k)
        for i, q, u, d, x, s, e, k in zip(inner, qs, us, ds, dvs, ss, both, ks)
    ]

    def through(grad, pair):
        unit, scale = pair
        return scale * (grad - unit * jnp.sum(unit * grad, -1, keepdims=True))

    dz = []
    for i, h in enumerate(every):
        put(0, h, through(dqn[i], qp[i]).astype(jnp.bfloat16))
        put(1, h, through(dkn[i], kp[i]).astype(jnp.bfloat16))
        put(2, h, dv[i].astype(jnp.bfloat16))
        dz.append(jnp.sum(dx[i] * plain[i], -1, keepdims=True) * beta[i] * (1.0 - 0.5 * beta[i]))
    return dz


def strength_lanes(heads, dz):
    lane = lax.broadcasted_iota(jnp.int32, (dz[0].shape[0], LANES), 1)
    last = jnp.zeros((dz[0].shape[0], LANES), jnp.float32)
    for h in range(heads):
        high, low = split(dz[h])
        last = jnp.where(lane == h, high.astype(jnp.float32), last)
        last = jnp.where(lane == heads + h, low.astype(jnp.float32), last)
    return last.astype(jnp.bfloat16)


def gradient_kernel(heads, dim, q_ref, k_ref, z_ref, g_ref, mid_ref, state_ref, out_ref):
    width = heads * dim

    def put(i, h, value):
        out_ref[:, i * width + h * dim : i * width + (h + 1) * dim] = value

    dz = gradients(
        heads, dim, range(heads), q_ref, k_ref, z_ref, g_ref, mid_ref,
        lambda unit: state_ref[unit], put,
    )
    out_ref[:, 3 * width :] = strength_lanes(heads, dz)


def gathered_states(maps, heads):
    count = lax.axis_size("seq")
    place = lax.axis_index("seq")
    gathered = lax.all_gather(maps, "seq").astype(jnp.float32)

    def walk(steps, pick, rows):
        def one(lap, state):
            pair = lax.dynamic_index_in_dim(gathered, pick(lap), 0, False)[rows]
            moved = jnp.einsum("hij,hjk->hik", state, pair[:, 0], precision=highest)
            return state - moved + pair[:, 1]

        return lax.fori_loop(0, steps, one, jnp.zeros((heads,) + maps.shape[2:], jnp.float32))

    first = walk(place, lambda lap: lap, slice(0, heads))
    second = walk(count - 1 - place, lambda lap: count - 1 - lap, slice(heads, None))
    return jnp.concatenate([first, second]).astype(maps.dtype)


def layer_kernel(
    groups, heads, dim,
    x_hbm, wq_hbm, wk_hbm, wv_hbm, g_hbm, wb_ref, b_ref,
    dx_ref, gq_ref, gk_ref, gv_ref, tail_ref,
    x, w, wb, g, qkv, z, mid, maps, x_out, x_in, y_out, y_in, state,
    cols, cols_t, mine, blocks, tails, part_out, part_in, tail_out, tail_in,
    own, piece, landed, relay,
    load, tok_send, tok_recv, map_send, map_recv, x_send, x_recv, f_send, f_recv,
    y_send, y_recv, far_send, far_recv, sib_send, sib_recv, fwd_send, fwd_recv,
    part_send, part_recv, z_send, z_recv, relay_recv,
):
    me = lax.axis_index("seq")
    group = lax.axis_index("head")
    core, across, upper = me % 2, (me // 2) % 2, me // 4
    rows, width = g.shape
    part = cols.shape[-1]
    half = heads // 2
    f32, bf16 = jnp.float32, jnp.bfloat16

    def seq(o):
        index = me
        for bit in (1, 2, 4):
            if o & bit:
                index = index + bit - 2 * bit * ((me // bit) % 2)
        return index

    def remote(source, target, send, recv, device):
        return pltpu.make_async_remote_copy(
            src_ref=source,
            dst_ref=target,
            send_sem=send,
            recv_sem=recv,
            device_id=device if isinstance(device, dict) else {"seq": seq(device)},
            device_id_type=MESH,
        )

    pairs = ((x_hbm, x), (wq_hbm, w.at[0]), (wk_hbm, w.at[1]), (wv_hbm, w.at[2]), (g_hbm, g))
    loads = [pltpu.make_async_copy(s, t, load.at[i]) for i, (s, t) in enumerate(pairs)]
    for copy in loads:
        copy.start()
    barrier = pltpu.get_barrier_semaphore()
    others = [{"seq": seq(o)} for o in range(1, 8)]
    others += [{"head": lax.rem(group + r, groups)} for r in range(1, groups)]
    for peer in others:
        pl.semaphore_signal(barrier, inc=1, device_id=peer, device_id_type=MESH)
    wb[...] = jnp.zeros_like(wb)
    wb[pl.ds(0, heads), :] = wb_ref[...]
    loads[0].wait()
    loads[1].wait()
    qkv[0] = dot(x[...], w[0])
    pl.semaphore_wait(barrier, len(others))

    fars, partners = (2, 4), (4, 2)
    slots = [(0, 1, far, far ^ 1) for far in fars]

    def columns(index):
        return pl.ds(pl.multiple_of(index * part, part), part)

    tokens = []
    for a in range(2):
        for s in range(1, 4):
            for b in range(2):
                if (a, s, b) != (1, 1, 0):
                    owner = seq(slots[a][s] ^ (partners[a] if b else 0))
                    i = len(tokens)
                    tokens.append(
                        remote(
                            x.at[:, columns(owner)], cols.at[a, s, b],
                            tok_send.at[i], tok_recv.at[i], slots[a][s],
                        )
                    )
                    tokens[i].start()

    loads[2].wait()
    qkv[1] = dot(x[...], w[1])
    loads[3].wait()
    qkv[2] = dot(x[...], w[2])
    z[...] = dot(x[...], wb[...], (1, 1))
    z[:, :heads] = z[:, :heads] + b_ref[...]
    loads[4].wait()

    def put_map(unit, factor, offset):
        maps[core, unit, 0] = factor.astype(bf16)
        maps[core, unit, 1] = offset.astype(bf16)

    put_mid = summarise(heads, dim, qkv.at[0], qkv.at[1], qkv.at[2], z, g, put_map)
    sibling = remote(maps.at[core], maps.at[core], map_send, map_recv, 1)
    sibling.start()
    put_mid(mid)
    sibling.wait_recv()

    passed, taken = across, 1 - across
    kept = pl.ds(core * half, half)

    def chip_total(way, n):
        unit = way * heads + core * half + n
        first = jnp.concatenate([maps[way, unit, 0], maps[way, unit, 1]], 0)
        factor = maps[1 - way, unit, 0]
        moved = dot(first, factor)
        both = first.astype(f32) - moved
        return both[:dim] + factor.astype(f32), both[dim:] + maps[1 - way, unit, 1].astype(f32)

    for n in range(half):
        factor, offset = chip_total(passed, n)
        x_out[0, n] = offset.astype(bf16)
        x_out[1, n] = factor.astype(bf16)
    over = [remote(x_out.at[j], x_in.at[j, kept], x_send.at[j], x_recv.at[j], 2) for j in range(2)]
    for copy in over:
        copy.start()
    totals = [chip_total(taken, n) for n in range(half)]
    forward = [
        remote(x_in.at[j, kept], x_in.at[j, kept], f_send.at[j], f_recv.at[j], 1) for j in range(2)
    ]

    def turn(a):
        far, partner = fars[a], partners[a]
        for s in range(4):
            for b in range(2):
                if s == 0:
                    block = x[:, columns(seq(partner) if b else me)]
                else:
                    block = cols[0, 1, 0] if (a, s, b) == (1, 1, 0) else cols[a, s, b]
                cols_t[a, b * part : (b + 1) * part, s * rows : (s + 1) * rows] = block.T

    for copy in tokens:
        copy.wait_recv()
    turn(0)
    over[0].wait_recv()
    for n, (factor, offset) in enumerate(totals):
        entering = x_in[0, core * half + n]
        y_out[n] = (entering.astype(f32) - mm((entering, None), split(factor)) + offset).astype(bf16)
    up = [
        remote(y_out, y_in.at[kept], y_send.at[j], y_recv.at[core], 4 + j) for j in range(4)
    ]

    @pl.when(upper == taken)
    def _():
        for copy in up:
            copy.start()

    forward[0].start()
    over[1].wait_recv()
    forward[1].start()
    turn(1)
    for copy in forward:
        copy.wait_recv()
    for c in range(2):
        remote(
            y_out, y_in.at[pl.ds(c * half, half)], y_send.at[0], y_recv.at[c], 4
        ).wait_recv()
    state[...] = jnp.zeros_like(state)
    for h in range(heads):
        state[(1 - upper) * heads + h] = y_in[h].astype(f32)

    def advance(unit, factor, offset):
        before = state[unit]
        state[unit] = before - mm(split(before), (factor, None)) + offset.astype(f32)

    for h in range(heads):
        advance(taken * heads + h, x_in[1, h], x_in[0, h])
    for h in range(heads):
        unit = (1 - core) * heads + h
        advance(unit, maps[1 - core, unit, 0], maps[1 - core, unit, 1])

    def put(i, h, value):
        a, n = h // half, h % half
        mine[:, i * width + h * dim : i * width + (h + 1) * dim] = value
        blocks[a, i, :rows, n * dim : (n + 1) * dim] = value

    def spread(a, i):
        held = blocks.at[a, i] if i < 3 else tails
        slot = [pl.ds(s * rows, rows) for s in range(4)]
        return (
            remote(held.at[slot[0]], held.at[slot[2]], far_send.at[a, i], far_recv.at[a, i], fars[a]),
            remote(held.at[slot[0]], held.at[slot[1]], sib_send.at[a, i], sib_recv.at[a, i], 1),
            remote(held.at[slot[2]], held.at[slot[3]], fwd_send.at[a, i], fwd_recv.at[a, i], 1),
        )

    def unit_state(unit):
        return state[unit].astype(bf16)

    spreads = {(a, i): spread(a, i) for a in range(2) for i in range(3)}
    spreads[0, 3] = spread(0, 3)
    dz = []
    for a in range(2):
        dz += gradients(
            heads, dim, range(a * half, (a + 1) * half),
            qkv.at[0], qkv.at[1], z, g, mid, unit_state, put,
        )
        for i in range(3):
            for copy in spreads[a, i][:2]:
                copy.start()
    last = strength_lanes(heads, dz)
    mine[:, 3 * width :] = last
    tails[:rows] = last
    for copy in spreads[0, 3][:2]:
        copy.start()

    def input_part(index):
        span = pl.ds(pl.multiple_of(index * width, width), width)
        total = dot(mine[:, 3 * width :], wb[:, span])
        for i in range(3):
            total = total + dot(mine[:, i * width : (i + 1) * width], w[i, span, :], (1, 1))
        return total

    side = 1 - 2 * (group // 2)
    edge = (group == 0) | (group == groups - 1)
    rim = jnp.where(edge, 1, 0)
    targets = [
        group + side * (1 + 2 * rim),
        group + side * (3 * rim - 1),
        group + side * (2 - rim),
    ]

    def landing(n):
        return remote(
            piece.at[n], landed.at[group], z_send.at[n], z_recv.at[group], {"head": targets[n]}
        )

    to_relay = remote(piece.at[0], relay, z_send.at[0], relay_recv, {"head": group + side})
    piece[0] = input_part(targets[0]).astype(bf16)

    @pl.when(edge)
    def _():
        to_relay.start()

    @pl.when(jnp.logical_not(edge))
    def _():
        landing(0).start()

    piece[1] = input_part(targets[1]).astype(bf16)

    @pl.when(jnp.logical_not(edge))
    def _():
        landing(1).start()

    piece[2] = input_part(targets[2]).astype(bf16)

    @pl.when(edge)
    def _():
        to_relay.wait_send()
        landing(1).start()
        landing(2).start()

    own[...] = input_part(group)

    grads = (gq_ref, gk_ref, gv_ref)
    order = [(a, i) for i in range(3) for a in range(2)] + [(0, 3)]
    trades = {
        (a, i): remote(
            part_out.at[a, i], part_in.at[a, i], part_send.at[a, i], part_recv.at[a, i], partners[a]
        )
        for a in range(2)
        for i in range(3)
    }
    tail_trade = remote(tail_out, tail_in, part_send.at[0, 3], part_recv.at[0, 3], partners[0])

    def process(a, i):
        spreads[a, i][1].wait_recv()
        spreads[a, i][2].wait_recv()
        if i < 3:
            value = dot(cols_t[a], blocks[a, i])
            part_out[a, i] = value[part:].astype(bf16)
            trades[a, i].start()
            grads[i][:, a * half * dim : (a + 1) * half * dim] = value[:part]
        else:
            value = dot(cols_t[a], tails[...]).T[:8]
            total = jnp.sum(tails[...].astype(f32), 0, keepdims=True)
            total = jnp.concatenate([total] * (part // LANES), 1)
            zero = jnp.zeros((7, part), f32)
            tail_out[...] = jnp.concatenate([value[:, part:], total, zero], 0)
            tail_trade.start()
            tail_ref[...] = jnp.concatenate([value[:, :part], total, zero], 0)

    for n, key in enumerate(order):
        spreads[key][0].wait_recv()
        spreads[key][2].start()
        if n > 0:
            process(*order[n - 1])
        if n == 3:

            @pl.when(jnp.logical_not(edge))
            def _():
                to_relay.wait_recv()
                piece[2] = (piece[2].astype(f32) + relay[...].astype(f32)).astype(bf16)
                landing(2).start()

    process(*order[-1])
    for a, i in order:
        if i < 3:
            trades[a, i].wait_recv()
            span = slice(a * half * dim, (a + 1) * half * dim)
            grads[i][:, span] = grads[i][:, span] + part_in[a, i].astype(f32)
    tail_trade.wait_recv()
    tail_ref[...] = tail_ref[...] + tail_in[...]

    def arrived(sender):
        remote(
            piece.at[0], landed.at[sender], z_send.at[0], z_recv.at[sender], {"head": targets[0]}
        ).wait_recv()
        return landed[sender].astype(f32)

    @pl.when(jnp.logical_not(edge))
    def _():
        own[...] = own[...] + arrived(group - side)

    dx_ref[...] = (own[...] + arrived(group + side) + arrived(group + 2 * side)).astype(bf16)
    sibling.wait_send()

    @pl.when(upper == taken)
    def _():
        for copy in up:
            copy.wait_send()

    @pl.when(jnp.logical_not(edge))
    def _():
        landing(0).wait_send()

    for n in (1, 2):
        landing(n).wait_send()
    for copy in tokens + over + forward + [tail_trade] + list(trades.values()):
        copy.wait_send()
    for copies in spreads.values():
        for copy in copies:
            copy.wait_send()


def place_kernel(count, heads, *refs):
    sems = refs[-1]
    tail_ref, bias_ref = refs[count], refs[2 * count + 2]
    copies = [
        pltpu.make_async_copy(refs[i], refs[count + 1 + i], sems.at[i]) for i in range(count)
    ]
    for copy in copies:
        copy.start()
    refs[2 * count + 1][...] = tail_ref[:heads, :]
    bias_ref[...] = tail_ref[8:9, :heads] + tail_ref[8:9, heads : 2 * heads]
    for copy in copies:
        copy.wait()


def place(arrays, tail, heads):
    count = len(arrays)
    vmem = pl.BlockSpec(memory_space=pltpu.VMEM)
    return pl.pallas_call(
        functools.partial(place_kernel, count, heads),
        out_shape=tuple(jax.ShapeDtypeStruct(a.shape, a.dtype) for a in arrays)
        + (
            jax.ShapeDtypeStruct((heads, tail.shape[1]), tail.dtype),
            jax.ShapeDtypeStruct((1, heads), tail.dtype),
        ),
        in_specs=[vmem] * (count + 1),
        out_specs=(pl.BlockSpec(memory_space=pltpu.HBM),) * count + (vmem,) * 2,
        scratch_shapes=[pltpu.SemaphoreType.DMA((count,))],
        name="place",
    )(*arrays, tail)


def whole_layer(tokens, weights, w_beta, b_beta, d_out):
    shards, groups = lax.axis_size("seq"), lax.axis_size("head")
    rows, features = tokens.shape
    heads = w_beta.shape[1]
    width = weights[0].shape[1]
    dim = width // heads
    half = heads // 2
    part = features // shards
    f32, bf16 = jnp.float32, jnp.bfloat16
    vmem = pl.BlockSpec(memory_space=pltpu.VMEM)
    hbm = pl.BlockSpec(memory_space=pl.ANY)
    square = jax.ShapeDtypeStruct((part, width), f32)
    dma = pltpu.SemaphoreType.DMA
    outs = pl.pallas_call(
        functools.partial(layer_kernel, groups, heads, dim),
        out_shape=(
            jax.ShapeDtypeStruct((rows, features // groups), tokens.dtype),
            square,
            square,
            square,
            jax.ShapeDtypeStruct((16, part), f32),
        ),
        in_specs=[hbm] * 5 + [vmem] * 2,
        out_specs=(vmem,) * 5,
        scratch_shapes=[
            pltpu.VMEM((rows, features), bf16),
            pltpu.VMEM((3, features, width), bf16),
            pltpu.VMEM((LANES, features), bf16),
            pltpu.VMEM((rows, width), bf16),
            pltpu.VMEM((3, rows, width), f32),
            pltpu.VMEM((rows, LANES), f32),
            pltpu.VMEM((heads, rows, 4 * dim), f32),
            pltpu.VMEM((2, 2 * heads, 2, dim, dim), bf16),
            pltpu.VMEM((2, half, dim, dim), bf16),
            pltpu.VMEM((2, heads, dim, dim), bf16),
            pltpu.VMEM((half, dim, dim), bf16),
            pltpu.VMEM((heads, dim, dim), bf16),
            pltpu.VMEM((2 * heads, dim, dim), f32),
            pltpu.VMEM((2, 4, 2, rows, part), bf16),
            pltpu.VMEM((2, 2 * part, 4 * rows), bf16),
            pltpu.VMEM((rows, 3 * width + LANES), bf16),
            pltpu.VMEM((2, 3, 4 * rows, width // 2), bf16),
            pltpu.VMEM((4 * rows, LANES), bf16),
            pltpu.VMEM((2, 3, part, width // 2), bf16),
            pltpu.VMEM((2, 3, part, width // 2), bf16),
            pltpu.VMEM((16, part), f32),
            pltpu.VMEM((16, part), f32),
            pltpu.VMEM((rows, features // groups), f32),
            pltpu.VMEM((3, rows, features // groups), bf16),
            pltpu.VMEM((groups, rows, features // groups), bf16),
            pltpu.VMEM((rows, features // groups), bf16),
            dma((5,)),
            dma((11,)),
            dma((11,)),
            dma,
            dma,
            dma((2,)),
            dma((2,)),
            dma((2,)),
            dma((2,)),
            dma((4,)),
            dma((2,)),
            dma((2, 4)),
            dma((2, 4)),
            dma((2, 4)),
            dma((2, 4)),
            dma((2, 4)),
            dma((2, 4)),
            dma((2, 4)),
            dma((2, 4)),
            dma((3,)),
            dma((groups,)),
            dma,
        ],
        compiler_params=pltpu.CompilerParams(
            vmem_limit_bytes=52 * 1024 * 1024, collective_id=1, has_side_effects=True
        ),
        name="layer",
    )(tokens, *weights, d_out, w_beta.T, b_beta.reshape(1, heads))
    d_x, grad_q, grad_k, grad_v, tail, bias = place(outs[:4], outs[4], heads)
    return d_x, grad_q, grad_k, grad_v, tail.T, bias.reshape(heads)


def per_device(tokens, w_query, w_key, w_value, w_beta, b_beta, d_out):
    token_count, features = tokens.shape
    heads = w_beta.shape[1]
    width = w_query.shape[1]
    dim = width // heads
    f32 = jnp.float32
    shards, groups = lax.axis_size("seq"), lax.axis_size("head")
    weights = (w_query, w_key, w_value)
    fits = heads % 2 == 0 and 2 * heads <= 8 and width * groups == features and dim == LANES
    if shards == 8 and groups == 4 and fits and features // shards == token_count:
        return whole_layer(tokens, weights, w_beta, b_beta, d_out)
    q, k, v = (jnp.dot(tokens, w, preferred_element_type=f32) for w in weights)
    w_last = jnp.pad(w_beta, ((0, 0), (0, LANES - heads)))
    z = jnp.dot(tokens, w_last, preferred_element_type=f32) + jnp.pad(b_beta, (0, LANES - heads))
    params = pltpu.CompilerParams(vmem_limit_bytes=60 * 1024 * 1024)
    columns = lax.all_to_all(tokens, "seq", split_axis=1, concat_axis=0, tiled=True)
    maps, mid = pl.pallas_call(
        functools.partial(summary_kernel, heads, dim),
        out_shape=(
            jax.ShapeDtypeStruct((2 * heads, 2, dim, dim), jnp.bfloat16),
            jax.ShapeDtypeStruct((heads, token_count, 4 * dim), f32),
        ),
        compiler_params=params,
        name="summary",
    )(q, k, v, z, d_out)
    states = gathered_states(maps, heads)
    grads = pl.pallas_call(
        functools.partial(gradient_kernel, heads, dim),
        out_shape=jax.ShapeDtypeStruct((token_count, 3 * width + LANES), jnp.bfloat16),
        compiler_params=params,
        name="gradient",
    )(q, k, z, d_out, mid, states)
    whole = lax.all_gather(grads, "seq", axis=0, tiled=True)
    partial = jnp.dot(grads[:, 3 * width : 3 * width + heads], w_beta.T, preferred_element_type=f32)
    for i, w in enumerate(weights):
        partial = partial + jnp.dot(
            grads[:, i * width : (i + 1) * width], w.T, preferred_element_type=f32
        )
    d_x = lax.psum_scatter(
        partial.astype(jnp.bfloat16), "head", scatter_dimension=1, tiled=True
    )

    def weight_grad(block):
        return lax.dot_general(
            columns, block, (((0,), (0,)), ((), ())), preferred_element_type=f32
        )

    found = [weight_grad(whole[:, i * width : (i + 1) * width]) for i in range(3)]
    tail = whole[:, 3 * width :]
    grad_wbeta = weight_grad(tail)[:, :heads]
    sums = jnp.sum(tail.astype(f32), 0)
    return (d_x, *found, grad_wbeta, sums[:heads] + sums[heads : 2 * heads])


def solution(mesh):
    in_specs = (
        P("seq", None),
        P(None, "head"),
        P(None, "head"),
        P(None, "head"),
        P(None, "head"),
        P("head"),
        P("seq", "head"),
    )
    out_specs = (
        P("seq", "head"),
        P("seq", "head"),
        P("seq", "head"),
        P("seq", "head"),
        P("seq", "head"),
        P("head"),
    )
    return jax.shard_map(
        per_device, mesh=mesh, in_specs=in_specs, out_specs=out_specs, check_vma=False
    )
```

time: 99.1 us -> 61.9 us (0.62)
  Pallas kernels: 85 us -> 55.6 us
  matrix products: 6.95 us -> 0 us
  other arithmetic: 1.26 us -> 0 us
    pallas_call x5 -> x2, Pallas kernels: 85 us -> 55.6 us  [the longest x1 52.4 us: whole_layer(): pl.pallas_call(functools.partial(layer_kernel, groups, heads, dim), out_s...]
    dot_general x4 -> x0, matrix products: 6.95 us -> none  [the longest x1 2.46 us: per_device(): jnp.dot(tokens, w_last, preferred_element_type=f32)]
    unnamed x10 -> x14, local copies, waits for them, and re-layouts: 2.8 us -> 5.2 us
    pad x2 -> x0, local copies, waits for them, and re-layouts: 1.63 us -> none  [the longest x1 0.88 us: per_device(): w_last = jnp.pad(w_beta, ((0, 0), (0, LANES - heads)))]
    add x1 -> x0, other arithmetic: 1.26 us -> none  [per_device(): bias = sums[0, :heads] + sums[0, heads:2 * heads]]
where the time goes in v1:
time: 61.9 us; the launch traced here: 61.7 us
  Pallas kernels  55.6 us (90%)
  local copies, waits for them, and re-layouts  5.2 us (8%)
  between operations  0.82 us (1%)
    pallas_call x1, Pallas kernels, whole_layer(): pl.pallas_call(functools.partial(layer_kernel, groups, heads, dim), out_s...  52.4 us
    unnamed x14, local copies, waits for them, and re-layouts  5.2 us
    pallas_call x1, Pallas kernels, place(): pl.pallas_call(functools.partial(place_kernel, count, heads), out_shape=t...  3.29 us

profile of v1, /device:TPU:0, one launch (start us, length us, event | category | flops | bytes accessed | tf_op | source)
XLA Modules:
  0.0 61.7 jit_solution(113576016043969103)
XLA Ops:
  0.6 0.0 copy-start.2
  0.6 0.9 %copy-done.2 = bf16[256,512]{1,0:T(8,128)(2,1)S(1)} copy-done((bf16[256,512]{1,0:T(8,128)(2,1)S(1)}, bf16[256,512]{1,0:T(8,128)(2,1)}, u32[]{:S(2)}) %copy-start.2) | copy-done | bytes 262168
  1.6 0.0 copy-start.4
  1.6 0.7 %copy-done.4 = bf16[2048,4]{0,1:T(4,128)(2,1)S(1)} copy-done((bf16[2048,4]{0,1:T(4,128)(2,1)S(1)}, bf16[2048,4]{0,1:T(4,128)(2,1)}, u32[]{:S(2)}) %copy-start.4) | copy-done | bytes 16408
  2.3 0.0 copy-start.6
  2.3 0.7 %copy-done.6 = f32[4]{0:T(128)S(1)} copy-done((f32[4]{0:T(128)S(1)}, f32[4]{0:T(128)}, u32[]{:S(2)}) %copy-start.6) | copy-done | bytes 40
  3.0 52.4 %layer.1 = (bf16[256,512]{1,0:T(8,128)(2,1)S(1)}, f32[256,512]{1,0:T(8,128)S(1)}, f32[256,512]{1,0:T(8,128)S(1)}, f32[256,512]{1,0:T(8,128)}, f32[16,256]{1,0:T(8,128)S(1)}) custom-call(bf16[256,2048]{1,0:T(8,128)(2,1)} %x_hbm.1, bf16[2048,512]{1,0:T(8,128)(2,1)} %wq_hbm.1, bf16[2048,512]{1,0:T(8,128)(2,1)} %wk_hbm.1, bf16[2048,512]{1,0:T(8,128)(2,1)} %wv_hbm.1, ...), custom_call_target="tpu_custom_call" | custom-call | tf_op jit(solution)/shard_map/layer/pallas_call | solution.py:608
  55.3 0.0 copy-start
  55.3 0.8 %copy-done = f32[256,512]{1,0:T(8,128)} copy-done((f32[256,512]{1,0:T(8,128)}, f32[256,512]{1,0:T(8,128)S(1)}, u32[]{:S(2)}) %copy-start) | copy-done | bytes 524312
  56.1 0.0 copy-start.1
  56.1 0.8 %copy-done.1 = f32[256,512]{1,0:T(8,128)} copy-done((f32[256,512]{1,0:T(8,128)}, f32[256,512]{1,0:T(8,128)S(1)}, u32[]{:S(2)}) %copy-start.1) | copy-done | bytes 524312
  56.9 0.0 copy-start.3
  56.9 0.7 %copy-done.3 = bf16[256,512]{1,0:T(8,128)(2,1)} copy-done((bf16[256,512]{1,0:T(8,128)(2,1)}, bf16[256,512]{1,0:T(8,128)(2,1)S(1)}, u32[]{:S(2)}) %copy-start.3) | copy-done | bytes 262168
  57.6 0.0 copy-start.5
  57.6 0.6 copy-done.5
  58.2 3.3 %place.1 = (bf16[256,512]{1,0:T(8,128)(2,1)}, f32[256,512]{1,0:T(8,128)}, f32[256,512]{1,0:T(8,128)}, f32[256,512]{1,0:T(8,128)}, f32[4,256]{1,0:T(4,128)}, /*index=5*/f32[1,4]{1,0:T(1,128)}) custom-call(bf16[256,512]{1,0:T(8,128)(2,1)} %copy-done.3, f32[256,512]{1,0:T(8,128)} %copy-done, f32[256,512]{1,0:T(8,128)} %copy-done.1, ...), custom_call_target="tpu_custom_call" | custom-call | tf_op jit(solution)/shard_map/place/pallas_call | solution.py:581
Async XLA Ops:
  0.6 1.0 %copy-start.2 = (bf16[256,512]{1,0:T(8,128)(2,1)S(1)}, bf16[256,512]{1,0:T(8,128)(2,1)}, u32[]{:S(2)}) copy-start(bf16[256,512]{1,0:T(8,128)(2,1)} %g_hbm.1) | copy-start | bytes 786436
  1.6 0.7 %copy-start.4 = (bf16[2048,4]{0,1:T(4,128)(2,1)S(1)}, bf16[2048,4]{0,1:T(4,128)(2,1)}, u32[]{:S(2)}) copy-start(bf16[2048,4]{0,1:T(4,128)(2,1)} %param.11) | copy-start | bytes 49156
  2.3 0.7 %copy-start.6 = (f32[4]{0:T(128)S(1)}, f32[4]{0:T(128)}, u32[]{:S(2)}) copy-start(f32[4]{0:T(128)} %param.12) | copy-start | bytes 52
  55.3 0.8 %copy-start = (f32[256,512]{1,0:T(8,128)}, f32[256,512]{1,0:T(8,128)S(1)}, u32[]{:S(2)}) copy-start(f32[256,512]{1,0:T(8,128)S(1)} %get-tuple-element.18.refs_1_) | copy-start | bytes 1572868
  56.1 0.8 %copy-start.1 = (f32[256,512]{1,0:T(8,128)}, f32[256,512]{1,0:T(8,128)S(1)}, u32[]{:S(2)}) copy-start(f32[256,512]{1,0:T(8,128)S(1)} %get-tuple-element.19.refs_2_) | copy-start | bytes 1572868
  56.9 0.7 %copy-start.3 = (bf16[256,512]{1,0:T(8,128)(2,1)}, bf16[256,512]{1,0:T(8,128)(2,1)S(1)}, u32[]{:S(2)}) copy-start(bf16[256,512]{1,0:T(8,128)(2,1)S(1)} %get-tuple-element.17.refs_0_) | copy-start | bytes 786436
  57.6 0.6 copy-start.5

commit v2 on v1

--- a/solution.py
+++ b/solution.py
@@ -146,13 +146,35 @@
     summarise(heads, dim, q_ref, k_ref, v_ref, z_ref, g_ref, put_map)(mid_ref)
 
 
-def gradients(heads, dim, every, q_ref, k_ref, z_ref, g_ref, mid_ref, state, put):
-    count = q_ref.shape[0]
-    row, col = iotas(count, count)
-    strict, inclusive = row > col, row >= col
+def value_gradients(heads, dim, q_ref, k_ref, z_ref, g_ref, mid_ref, state):
+    every = range(heads)
     beta_all = 2.0 * jax.nn.sigmoid(z_ref[...])
     cols = [slice(h * dim, (h + 1) * dim) for h in every]
     beta = [beta_all[:, h : h + 1] for h in every]
+    ds = [(state(heads + h), None) for h in every]
+    ss = [(state(h), None) for h in every]
+    dx = [
+        mid_ref[h, :, 2 * dim : 3 * dim] + mm(split(mid_ref[h, :, 3 * dim :]), d, (1, 1))
+        for h, d in zip(every, ds)
+    ]
+    dv = [b * x for b, x in zip(beta, dx)]
+    plain = [
+        mid_ref[h, :, :dim] - mm(split(mid_ref[h, :, dim : 2 * dim]), s, (1, 1))
+        for h, s in zip(every, ss)
+    ]
+    us = [split(b * x) for b, x in zip(beta, plain)]
+    dz = [
+        jnp.sum(x * p, -1, keepdims=True) * b * (1.0 - 0.5 * b) for x, p, b in zip(dx, plain, beta)
+    ]
+    return dv, us, dz
+
+
+def key_gradients(heads, dim, q_ref, k_ref, g_ref, state, dv, us, put, between):
+    every = range(heads)
+    count = q_ref.shape[0] // 2
+    row, col = iotas(count, count)
+    strict, inclusive = row > col, row >= col
+    cols = [slice(h * dim, (h + 1) * dim) for h in every]
     qp = [normalise(q_ref[:, c]) for c in cols]
     kp = [normalise(k_ref[:, c]) for c in cols]
     ks = [split(x[0]) for x in kp]
@@ -160,37 +182,56 @@
     gs = [(g_ref[:, c], None) for c in cols]
     ss = [(state(h), None) for h in every]
     ds = [(state(heads + h), None) for h in every]
-    plain = [
-        mid_ref[h, :, :dim] - mm(split(mid_ref[h, :, dim : 2 * dim]), s, (1, 1))
-        for h, s in zip(every, ss)
-    ]
-    dx = [
-        mid_ref[h, :, 2 * dim : 3 * dim] + mm(split(mid_ref[h, :, 3 * dim :]), d, (1, 1))
-        for h, d in zip(every, ds)
-    ]
-    us = [split(b * x) for b, x in zip(beta, plain)]
-    dv = [b * x for b, x in zip(beta, dx)]
     dvs = [split(x) for x in dv]
-    inner = [split(jnp.where(inclusive, mm(g, u, (1, 1)), 0.0)) for g, u in zip(gs, us)]
-    pair = [jnp.where(strict, mm(d, u, (1, 1)), 0.0) for d, u in zip(dvs, us)]
-    both = [split(e + e.T) for e in pair]
-    dqn = [mm(g, s) + mm(i, k) for g, s, i, k in zip(gs, ss, inner, ks)]
+
+    def top(x):
+        return tuple(None if y is None else y[:count] for y in x)
+
+    def low(x):
+        return tuple(None if y is None else y[count:] for y in x)
+
+    def masked(mask, x):
+        return jnp.concatenate([x[:, :count], jnp.where(mask, x[:, count:], 0.0)], 1)
+
+    inner_top = [split(jnp.where(inclusive, mm(top(g), top(u), (1, 1)), 0.0)) for g, u in zip(gs, us)]
+    pair_top = [jnp.where(strict, mm(top(d), top(u), (1, 1)), 0.0) for d, u in zip(dvs, us)]
+    inner_low = [split(masked(inclusive, mm(low(g), u, (1, 1)))) for g, u in zip(gs, us)]
+    pair_low = [masked(strict, mm(low(d), u, (1, 1))) for d, u in zip(dvs, us)]
+    both_top = [
+        split(jnp.concatenate([e + e.T, f[:, :count].T], 1)) for e, f in zip(pair_top, pair_low)
+    ]
+    both_low = [
+        split(jnp.concatenate([f[:, :count], f[:, count:] + f[:, count:].T], 1)) for f in pair_low
+    ]
+
+    def through(grad, pair, rows):
+        unit, scale = pair[0][rows], pair[1][rows]
+        return scale * (grad - unit * jnp.sum(unit * grad, -1, keepdims=True))
+
+    def finish(rows, dqn, dkn):
+        for h in every:
+            put(0, h, rows, through(dqn[h], qp[h], rows).astype(jnp.bfloat16))
+            put(1, h, rows, through(dkn[h], kp[h], rows).astype(jnp.bfloat16))
+
+    def left(x):
+        return tuple(y[:, :count] for y in x)
+
+    def right(x):
+        return tuple(y[:, count:] for y in x)
+
+    dqn = [mm(top(g), s) + mm(i, top(k)) for g, s, i, k in zip(gs, ss, inner_top, ks)]
     dkn = [
-        mm(i, q, (0, 0)) + mm(u, d) - mm(x, s) - mm(e, k)
-        for i, q, u, d, x, s, e, k in zip(inner, qs, us, ds, dvs, ss, both, ks)
-    ]
-
-    def through(grad, pair):
-        unit, scale = pair
-        return scale * (grad - unit * jnp.sum(unit * grad, -1, keepdims=True))
-
-    dz = []
-    for i, h in enumerate(every):
-        put(0, h, through(dqn[i], qp[i]).astype(jnp.bfloat16))
-        put(1, h, through(dkn[i], kp[i]).astype(jnp.bfloat16))
-        put(2, h, dv[i].astype(jnp.bfloat16))
-        dz.append(jnp.sum(dx[i] * plain[i], -1, keepdims=True) * beta[i] * (1.0 - 0.5 * beta[i]))
-    return dz
+        mm(i, top(q), (0, 0)) + mm(left(j), low(q), (0, 0)) + mm(top(u), d) - mm(top(x), s) - mm(e, k)
+        for i, j, q, u, d, x, s, e, k in zip(inner_top, inner_low, qs, us, ds, dvs, ss, both_top, ks)
+    ]
+    finish(slice(0, count), dqn, dkn)
+    between()
+    dqn = [mm(low(g), s) + mm(j, k) for g, s, j, k in zip(gs, ss, inner_low, ks)]
+    dkn = [
+        mm(right(j), low(q), (0, 0)) + mm(low(u), d) - mm(low(x), s) - mm(e, k)
+        for j, q, u, d, x, s, e, k in zip(inner_low, qs, us, ds, dvs, ss, both_low, ks)
+    ]
+    finish(slice(count, 2 * count), dqn, dkn)
 
 
 def strength_lanes(heads, dz):
@@ -200,20 +241,23 @@
         high, low = split(dz[h])
         last = jnp.where(lane == h, high.astype(jnp.float32), last)
         last = jnp.where(lane == heads + h, low.astype(jnp.float32), last)
-    return last.astype(jnp.bfloat16)
+    return last
 
 
 def gradient_kernel(heads, dim, q_ref, k_ref, z_ref, g_ref, mid_ref, state_ref, out_ref):
     width = heads * dim
 
-    def put(i, h, value):
-        out_ref[:, i * width + h * dim : i * width + (h + 1) * dim] = value
-
-    dz = gradients(
-        heads, dim, range(heads), q_ref, k_ref, z_ref, g_ref, mid_ref,
-        lambda unit: state_ref[unit], put,
-    )
-    out_ref[:, 3 * width :] = strength_lanes(heads, dz)
+    def put(i, h, rows, value):
+        out_ref[rows, i * width + h * dim : i * width + (h + 1) * dim] = value
+
+    def state(unit):
+        return state_ref[unit]
+
+    dv, us, dz = value_gradients(heads, dim, q_ref, k_ref, z_ref, g_ref, mid_ref, state)
+    for h in range(heads):
+        put(2, h, slice(None), dv[h].astype(jnp.bfloat16))
+    key_gradients(heads, dim, q_ref, k_ref, g_ref, state, dv, us, put, lambda: None)
+    out_ref[:, 3 * width :] = strength_lanes(heads, dz).astype(jnp.bfloat16)
 
 
 def gathered_states(maps, heads):
@@ -236,14 +280,14 @@
 
 def layer_kernel(
     groups, heads, dim,
-    x_hbm, wq_hbm, wk_hbm, wv_hbm, g_hbm, wb_ref, b_ref,
-    dx_ref, gq_ref, gk_ref, gv_ref, tail_ref,
-    x, w, wb, g, qkv, z, mid, maps, x_out, x_in, y_out, y_in, state,
+    x_hbm, wq_hbm, wk_hbm, wv_hbm, g_hbm, wb_hbm, b_hbm,
+    dx_hbm, gq_hbm, gk_hbm, gv_hbm, tail_hbm,
+    dx_ref, grads, tail_ref, x, w, wb, g, wb_ref, b_ref, qkv, z, mid, maps, x_out, x_in, y_out, y_in, state,
     cols, cols_t, mine, blocks, tails, part_out, part_in, tail_out, tail_in,
-    own, piece, landed, relay,
+    own, piece, landed,
     load, tok_send, tok_recv, map_send, map_recv, x_send, x_recv, f_send, f_recv,
-    y_send, y_recv, far_send, far_recv, sib_send, sib_recv, fwd_send, fwd_recv,
-    part_send, part_recv, z_send, z_recv, relay_recv,
+    y_send, y_recv, s_recv, far_send, far_recv, sib_send, sib_recv, fwd_send, fwd_recv,
+    part_send, part_recv, z_send, z_recv, save,
 ):
     me = lax.axis_index("seq")
     group = lax.axis_index("head")
@@ -270,7 +314,10 @@
             device_id_type=MESH,
         )
 
-    pairs = ((x_hbm, x), (wq_hbm, w.at[0]), (wk_hbm, w.at[1]), (wv_hbm, w.at[2]), (g_hbm, g))
+    pairs = (
+        (x_hbm, x), (wk_hbm, w.at[1]), (wb_hbm, wb_ref), (b_hbm, b_ref), (g_hbm, g),
+        (wq_hbm, w.at[0]), (wv_hbm, w.at[2]),
+    )
     loads = [pltpu.make_async_copy(s, t, load.at[i]) for i, (s, t) in enumerate(pairs)]
     for copy in loads:
         copy.start()
@@ -280,10 +327,6 @@
     for peer in others:
         pl.semaphore_signal(barrier, inc=1, device_id=peer, device_id_type=MESH)
     wb[...] = jnp.zeros_like(wb)
-    wb[pl.ds(0, heads), :] = wb_ref[...]
-    loads[0].wait()
-    loads[1].wait()
-    qkv[0] = dot(x[...], w[0])
     pl.semaphore_wait(barrier, len(others))
 
     fars, partners = (2, 4), (4, 2)
@@ -301,32 +344,55 @@
                     i = len(tokens)
                     tokens.append(
                         remote(
-                            x.at[:, columns(owner)], cols.at[a, s, b],
+                            x_hbm.at[:, columns(owner)], cols.at[a, s, b],
                             tok_send.at[i], tok_recv.at[i], slots[a][s],
                         )
                     )
                     tokens[i].start()
 
-    loads[2].wait()
+    loads[0].wait()
+    loads[1].wait()
     qkv[1] = dot(x[...], w[1])
-    loads[3].wait()
-    qkv[2] = dot(x[...], w[2])
+    for copy in loads[2:]:
+        copy.wait()
+    wb[pl.ds(0, heads), :] = wb_ref[...]
     z[...] = dot(x[...], wb[...], (1, 1))
     z[:, :heads] = z[:, :heads] + b_ref[...]
-    loads[4].wait()
+    qkv[0] = dot(x[...], w[0])
+    qkv[2] = dot(x[...], w[2])
 
     def put_map(unit, factor, offset):
         maps[core, unit, 0] = factor.astype(bf16)
         maps[core, unit, 1] = offset.astype(bf16)
 
     put_mid = summarise(heads, dim, qkv.at[0], qkv.at[1], qkv.at[2], z, g, put_map)
-    sibling = remote(maps.at[core], maps.at[core], map_send, map_recv, 1)
-    sibling.start()
+    passed, taken = across, 1 - across
+    kept, other = pl.ds(core * half, half), pl.ds((1 - core) * half, half)
+    urgent = [
+        (way * heads + n * half, j)
+        for j, (way, n) in enumerate(
+            [(passed, 1 - core), (taken, 1 - core), (passed, core), (taken, core)]
+        )
+    ]
+    sibling = [
+        remote(
+            maps.at[core, pl.ds(unit, half)], maps.at[core, pl.ds(unit, half)],
+            map_send.at[j], map_recv.at[j], 1,
+        )
+        for unit, j in urgent
+    ]
+    arriving = [
+        remote(
+            maps.at[1 - core, pl.ds(way * heads + n * half, half)],
+            maps.at[1 - core, pl.ds(way * heads + n * half, half)],
+            map_send.at[j], map_recv.at[j], 1,
+        )
+        for j, (way, n) in enumerate([(passed, core), (taken, core), (passed, 1 - core), (taken, 1 - core)])
+    ]
+    for copy in sibling:
+        copy.start()
     put_mid(mid)
-    sibling.wait_recv()
-
-    passed, taken = across, 1 - across
-    kept = pl.ds(core * half, half)
+    arriving[0].wait_recv()
 
     def chip_total(way, n):
         unit = way * heads + core * half + n
@@ -343,17 +409,20 @@
     over = [remote(x_out.at[j], x_in.at[j, kept], x_send.at[j], x_recv.at[j], 2) for j in range(2)]
     for copy in over:
         copy.start()
+    arriving[1].wait_recv()
     totals = [chip_total(taken, n) for n in range(half)]
     forward = [
         remote(x_in.at[j, kept], x_in.at[j, kept], f_send.at[j], f_recv.at[j], 1) for j in range(2)
     ]
 
+    def own_columns(a, b):
+        return x[:, columns(seq(partners[a]) if b else me)]
+
     def turn(a):
-        far, partner = fars[a], partners[a]
         for s in range(4):
             for b in range(2):
                 if s == 0:
-                    block = x[:, columns(seq(partner) if b else me)]
+                    block = own_columns(a, b)
                 else:
                     block = cols[0, 1, 0] if (a, s, b) == (1, 1, 0) else cols[a, s, b]
                 cols_t[a, b * part : (b + 1) * part, s * rows : (s + 1) * rows] = block.T
@@ -365,9 +434,8 @@
     for n, (factor, offset) in enumerate(totals):
         entering = x_in[0, core * half + n]
         y_out[n] = (entering.astype(f32) - mm((entering, None), split(factor)) + offset).astype(bf16)
-    up = [
-        remote(y_out, y_in.at[kept], y_send.at[j], y_recv.at[core], 4 + j) for j in range(4)
-    ]
+    up = [remote(y_out, y_in.at[kept], y_send.at[j], y_recv, 4 + 2 * j) for j in range(2)]
+    share = remote(y_in.at[kept], y_in.at[kept], y_send.at[2], s_recv, 1)
 
     @pl.when(upper == taken)
     def _():
@@ -378,38 +446,42 @@
     over[1].wait_recv()
     forward[1].start()
     turn(1)
-    for copy in forward:
+    for copy in forward + arriving[2:]:
         copy.wait_recv()
-    for c in range(2):
-        remote(
-            y_out, y_in.at[pl.ds(c * half, half)], y_send.at[0], y_recv.at[c], 4
-        ).wait_recv()
     state[...] = jnp.zeros_like(state)
     for h in range(heads):
-        state[(1 - upper) * heads + h] = y_in[h].astype(f32)
-
-    def advance(unit, factor, offset):
+        state[taken * heads + h] = x_in[0, h].astype(f32)
+    bridge = []
+    lead, inside = 1 - upper, 1 - core
+    for h in range(heads):
+        unit = inside * heads + h
+        factor = maps[inside, unit, 0]
         before = state[unit]
-        state[unit] = before - mm(split(before), (factor, None)) + offset.astype(f32)
-
+        state[unit] = before - mm(split(before), (factor, None)) + maps[inside, unit, 1].astype(f32)
+        first = jnp.where(taken == lead, x_in[1, h].astype(f32), 0.0).astype(bf16)
+        second = jnp.where(inside == lead, factor.astype(f32), 0.0).astype(bf16)
+        bridge.append(split(first.astype(f32) + second.astype(f32) - dot(first, second)))
+    up[0].wait_recv()
+    share.start()
+    share.wait_recv()
     for h in range(heads):
-        advance(taken * heads + h, x_in[1, h], x_in[0, h])
-    for h in range(heads):
-        unit = (1 - core) * heads + h
-        advance(unit, maps[1 - core, unit, 0], maps[1 - core, unit, 1])
-
-    def put(i, h, value):
+        unit = lead * heads + h
+        state[unit] = state[unit] + (y_in[h].astype(f32) - mm((y_in[h], None), bridge[h]))
+
+    def put(i, h, span, value):
         a, n = h // half, h % half
-        mine[:, i * width + h * dim : i * width + (h + 1) * dim] = value
-        blocks[a, i, :rows, n * dim : (n + 1) * dim] = value
+        mine[span, i * width + h * dim : i * width + (h + 1) * dim] = value
+        blocks[a, i, span, n * dim : (n + 1) * dim] = value
 
     def spread(a, i):
-        held = blocks.at[a, i] if i < 3 else tails
-        slot = [pl.ds(s * rows, rows) for s in range(4)]
+        if i < 3:
+            slot = [blocks.at[a, i, pl.ds(s * rows, rows)] for s in range(4)]
+        else:
+            slot = [tails.at[s] for s in range(4)]
         return (
-            remote(held.at[slot[0]], held.at[slot[2]], far_send.at[a, i], far_recv.at[a, i], fars[a]),
-            remote(held.at[slot[0]], held.at[slot[1]], sib_send.at[a, i], sib_recv.at[a, i], 1),
-            remote(held.at[slot[2]], held.at[slot[3]], fwd_send.at[a, i], fwd_recv.at[a, i], 1),
+            remote(slot[0], slot[2], far_send.at[a, i], far_recv.at[a, i], fars[a]),
+            remote(slot[0], slot[1], sib_send.at[a, i], sib_recv.at[a, i], 1),
+            remote(slot[2], slot[3], fwd_send.at[a, i], fwd_recv.at[a, i], 1),
         )
 
     def unit_state(unit):
@@ -417,26 +489,27 @@
 
     spreads = {(a, i): spread(a, i) for a in range(2) for i in range(3)}
     spreads[0, 3] = spread(0, 3)
-    dz = []
-    for a in range(2):
-        dz += gradients(
-            heads, dim, range(a * half, (a + 1) * half),
-            qkv.at[0], qkv.at[1], z, g, mid, unit_state, put,
-        )
+
+    def send(key):
+        for copy in spreads[key][:2]:
+            copy.start()
+
+    dv, us, dz = value_gradients(heads, dim, qkv.at[0], qkv.at[1], z, g, mid, unit_state)
+    for h in range(heads):
+        put(2, h, slice(0, rows), dv[h].astype(bf16))
+    send((0, 2))
+    send((1, 2))
+    last = strength_lanes(heads, dz)
+    mine[:, 3 * width :] = last.astype(bf16)
+    tails[0] = last.T[:16].astype(bf16)
+    send((0, 3))
+    halves = [slice(0, rows // 2), slice(rows // 2, rows)]
+
+    def input_part(index, rows):
+        span = pl.ds(pl.multiple_of(index * width, width), width)
+        total = dot(mine[rows, 3 * width :], wb[:, span])
         for i in range(3):
-            for copy in spreads[a, i][:2]:
-                copy.start()
-    last = strength_lanes(heads, dz)
-    mine[:, 3 * width :] = last
-    tails[:rows] = last
-    for copy in spreads[0, 3][:2]:
-        copy.start()
-
-    def input_part(index):
-        span = pl.ds(pl.multiple_of(index * width, width), width)
-        total = dot(mine[:, 3 * width :], wb[:, span])
-        for i in range(3):
-            total = total + dot(mine[:, i * width : (i + 1) * width], w[i, span, :], (1, 1))
+            total = total + dot(mine[rows, i * width : (i + 1) * width], w[i, span, :], (1, 1))
         return total
 
     side = 1 - 2 * (group // 2)
@@ -448,40 +521,50 @@
         group + side * (2 - rim),
     ]
 
-    def landing(n):
+    def landing(n, h):
+        slot = jnp.where(edge, groups, group) if n == 0 else group
+        device = group + side if n == 0 else targets[n]
         return remote(
-            piece.at[n], landed.at[group], z_send.at[n], z_recv.at[group], {"head": targets[n]}
+            piece.at[n, halves[h]], landed.at[slot, halves[h]],
+            z_send.at[n, h], z_recv.at[slot, h], {"head": device},
         )
 
-    to_relay = remote(piece.at[0], relay, z_send.at[0], relay_recv, {"head": group + side})
-    piece[0] = input_part(targets[0]).astype(bf16)
+    def first_piece(h):
+        piece[0, halves[h]] = input_part(targets[0], halves[h]).astype(bf16)
+        landing(0, h).start()
+
+    key_gradients(
+        heads, dim, qkv.at[0], qkv.at[1], g, unit_state, dv, us, put, lambda: first_piece(0)
+    )
+    for key in ((0, 0), (1, 0), (0, 1), (1, 1)):
+        send(key)
+    first_piece(1)
+    piece[1] = input_part(targets[1], slice(0, rows)).astype(bf16)
+    for h in range(2):
+        landing(1, h).start()
+    piece[2] = input_part(targets[2], slice(0, rows)).astype(bf16)
 
     @pl.when(edge)
     def _():
-        to_relay.start()
-
-    @pl.when(jnp.logical_not(edge))
-    def _():
-        landing(0).start()
-
-    piece[1] = input_part(targets[1]).astype(bf16)
-
-    @pl.when(jnp.logical_not(edge))
-    def _():
-        landing(1).start()
-
-    piece[2] = input_part(targets[2]).astype(bf16)
-
-    @pl.when(edge)
-    def _():
-        to_relay.wait_send()
-        landing(1).start()
-        landing(2).start()
-
-    own[...] = input_part(group)
-
-    grads = (gq_ref, gk_ref, gv_ref)
-    order = [(a, i) for i in range(3) for a in range(2)] + [(0, 3)]
+        for h in range(2):
+            landing(2, h).start()
+
+    own[...] = input_part(group, slice(0, rows))
+
+    def arrived(slot, h):
+        remote(
+            piece.at[0, halves[h]], landed.at[slot, halves[h]],
+            z_send.at[0, h], z_recv.at[slot, h], {"head": targets[0]},
+        ).wait_recv()
+        return landed[slot, halves[h]].astype(f32)
+
+    def pass_on(h):
+        @pl.when(jnp.logical_not(edge))
+        def _():
+            piece[2, halves[h]] = (piece[2, halves[h]].astype(f32) + arrived(groups, h)).astype(bf16)
+            landing(2, h).start()
+
+    order = [(0, 2), (1, 2), (0, 3), (0, 0), (1, 0), (0, 1), (1, 1)]
     trades = {
         (a, i): remote(
             part_out.at[a, i], part_in.at[a, i], part_send.at[a, i], part_recv.at[a, i], partners[a]
@@ -498,86 +581,102 @@
             value = dot(cols_t[a], blocks[a, i])
             part_out[a, i] = value[part:].astype(bf16)
             trades[a, i].start()
-            grads[i][:, a * half * dim : (a + 1) * half * dim] = value[:part]
+            grads[i, :, a * half * dim : (a + 1) * half * dim] = value[:part]
         else:
-            value = dot(cols_t[a], tails[...]).T[:8]
-            total = jnp.sum(tails[...].astype(f32), 0, keepdims=True)
-            total = jnp.concatenate([total] * (part // LANES), 1)
-            zero = jnp.zeros((7, part), f32)
-            tail_out[...] = jnp.concatenate([value[:, part:], total, zero], 0)
+            sums = [dot(tails[0], own_columns(0, b)) for b in range(2)]
+            for s in range(1, 4):
+                sums = [t + dot(tails[s], cols[0, s, b]) for b, t in enumerate(sums)]
+            held = jnp.sum(tails[...].astype(f32), 0)
+            held = jnp.sum(held, -1, keepdims=True)
+            row, col = iotas(16, part)
+            held = jnp.sum(jnp.where(row == col, held, 0.0), 0, keepdims=True)
+            row = lax.broadcasted_iota(jnp.int32, (16, part), 0)
+            tail_out[...] = jnp.where(row == 8, held, sums[1])
             tail_trade.start()
-            tail_ref[...] = jnp.concatenate([value[:, :part], total, zero], 0)
+            tail_ref[...] = jnp.where(row == 8, held, sums[0])
 
     for n, key in enumerate(order):
         spreads[key][0].wait_recv()
         spreads[key][2].start()
         if n > 0:
             process(*order[n - 1])
-        if n == 3:
-
-            @pl.when(jnp.logical_not(edge))
-            def _():
-                to_relay.wait_recv()
-                piece[2] = (piece[2].astype(f32) + relay[...].astype(f32)).astype(bf16)
-                landing(2).start()
+        if n == 2:
+            pass_on(0)
+        if n == 4:
+            pass_on(1)
 
     process(*order[-1])
+    saves = []
+
+    def keep(source, target):
+        copy = pltpu.make_async_copy(source, target, save.at[len(saves)])
+        copy.start()
+        saves.append(copy)
+
+    targets_hbm = (gq_hbm, gk_hbm, gv_hbm)
     for a, i in order:
         if i < 3:
             trades[a, i].wait_recv()
             span = slice(a * half * dim, (a + 1) * half * dim)
-            grads[i][:, span] = grads[i][:, span] + part_in[a, i].astype(f32)
-    tail_trade.wait_recv()
-    tail_ref[...] = tail_ref[...] + tail_in[...]
-
-    def arrived(sender):
-        remote(
-            piece.at[0], landed.at[sender], z_send.at[0], z_recv.at[sender], {"head": targets[0]}
-        ).wait_recv()
-        return landed[sender].astype(f32)
-
-    @pl.when(jnp.logical_not(edge))
-    def _():
-        own[...] = own[...] + arrived(group - side)
-
-    dx_ref[...] = (own[...] + arrived(group + side) + arrived(group + 2 * side)).astype(bf16)
-    sibling.wait_send()
+            grads[i, :, span] = grads[i, :, span] + part_in[a, i].astype(f32)
+            keep(grads.at[i, :, span], targets_hbm[i].at[:, span])
+        else:
+            tail_trade.wait_recv()
+            tail_ref[...] = tail_ref[...] + tail_in[...]
+            keep(tail_ref, tail_hbm)
+
+    for h in range(2):
+
+        @pl.when(jnp.logical_not(edge))
+        def _():
+            own[halves[h]] = own[halves[h]] + arrived(group - side, h)
+
+        total = own[halves[h]] + arrived(group + side, h) + arrived(group + 2 * side, h)
+        dx_ref[halves[h]] = total.astype(bf16)
+        keep(dx_ref.at[halves[h]], dx_hbm.at[halves[h]])
+
+    share.wait_send()
 
     @pl.when(upper == taken)
     def _():
         for copy in up:
             copy.wait_send()
 
-    @pl.when(jnp.logical_not(edge))
-    def _():
-        landing(0).wait_send()
-
-    for n in (1, 2):
-        landing(n).wait_send()
-    for copy in tokens + over + forward + [tail_trade] + list(trades.values()):
+    for n in range(3):
+        for h in range(2):
+            landing(n, h).wait_send()
+    for copy in sibling + tokens + over + forward + [tail_trade] + list(trades.values()):
         copy.wait_send()
     for copies in spreads.values():
         for copy in copies:
             copy.wait_send()
+    for copy in saves:
+        copy.wait()
 
 
 def place_kernel(count, heads, *refs):
-    sems = refs[-1]
-    tail_ref, bias_ref = refs[count], refs[2 * count + 2]
-    copies = [
-        pltpu.make_async_copy(refs[i], refs[count + 1 + i], sems.at[i]) for i in range(count)
-    ]
-    for copy in copies:
+    sources, outs = refs[: count + 1], refs[count + 1 : 2 * count + 3]
+    held, sems = refs[2 * count + 3 : -1], refs[-1]
+    fetch = [
+        pltpu.make_async_copy(sources[i], held[i], sems.at[0, i]) for i in range(count + 1)
+    ]
+    store = [pltpu.make_async_copy(held[i], outs[i], sems.at[1, i]) for i in range(count)]
+    for copy in fetch:
         copy.start()
-    refs[2 * count + 1][...] = tail_ref[:heads, :]
-    bias_ref[...] = tail_ref[8:9, :heads] + tail_ref[8:9, heads : 2 * heads]
-    for copy in copies:
+    for i in range(count):
+        fetch[i].wait()
+        store[i].start()
+    fetch[count].wait()
+    outs[count][...] = held[count][:heads, :]
+    outs[count + 1][...] = held[count][8:9, :heads] + held[count][8:9, heads : 2 * heads]
+    for copy in store:
         copy.wait()
 
 
 def place(arrays, tail, heads):
     count = len(arrays)
     vmem = pl.BlockSpec(memory_space=pltpu.VMEM)
+    hbm = pl.BlockSpec(memory_space=pltpu.HBM)
     return pl.pallas_call(
         functools.partial(place_kernel, count, heads),
         out_shape=tuple(jax.ShapeDtypeStruct(a.shape, a.dtype) for a in arrays)
@@ -585,9 +684,11 @@
             jax.ShapeDtypeStruct((heads, tail.shape[1]), tail.dtype),
             jax.ShapeDtypeStruct((1, heads), tail.dtype),
         ),
-        in_specs=[vmem] * (count + 1),
-        out_specs=(pl.BlockSpec(memory_space=pltpu.HBM),) * count + (vmem,) * 2,
-        scratch_shapes=[pltpu.SemaphoreType.DMA((count,))],
+        in_specs=[hbm] * (count + 1),
+        out_specs=(hbm,) * count + (vmem,) * 2,
+        scratch_shapes=[pltpu.VMEM(a.shape, a.dtype) for a in (*arrays, tail)]
+        + [pltpu.SemaphoreType.DMA((2, count + 1))],
+        compiler_params=pltpu.CompilerParams(vmem_limit_bytes=60 * 1024 * 1024),
         name="place",
     )(*arrays, tail)
 
@@ -601,8 +702,7 @@
     half = heads // 2
     part = features // shards
     f32, bf16 = jnp.float32, jnp.bfloat16
-    vmem = pl.BlockSpec(memory_space=pltpu.VMEM)
-    hbm = pl.BlockSpec(memory_space=pl.ANY)
+    hbm = pl.BlockSpec(memory_space=pltpu.HBM)
     square = jax.ShapeDtypeStruct((part, width), f32)
     dma = pltpu.SemaphoreType.DMA
     outs = pl.pallas_call(
@@ -614,13 +714,18 @@
             square,
             jax.ShapeDtypeStruct((16, part), f32),
         ),
-        in_specs=[hbm] * 5 + [vmem] * 2,
-        out_specs=(vmem,) * 5,
+        in_specs=[hbm] * 7,
+        out_specs=(hbm,) * 5,
         scratch_shapes=[
+            pltpu.VMEM((rows, features // groups), bf16),
+            pltpu.VMEM((3, part, width), f32),
+            pltpu.VMEM((16, part), f32),
             pltpu.VMEM((rows, features), bf16),
             pltpu.VMEM((3, features, width), bf16),
             pltpu.VMEM((LANES, features), bf16),
             pltpu.VMEM((rows, width), bf16),
+            pltpu.VMEM((heads, features), bf16),
+            pltpu.VMEM((1, heads), f32),
             pltpu.VMEM((3, rows, width), f32),
             pltpu.VMEM((rows, LANES), f32),
             pltpu.VMEM((heads, rows, 4 * dim), f32),
@@ -634,26 +739,26 @@
             pltpu.VMEM((2, 2 * part, 4 * rows), bf16),
             pltpu.VMEM((rows, 3 * width + LANES), bf16),
             pltpu.VMEM((2, 3, 4 * rows, width // 2), bf16),
-            pltpu.VMEM((4 * rows, LANES), bf16),
+            pltpu.VMEM((4, 16, rows), bf16),
             pltpu.VMEM((2, 3, part, width // 2), bf16),
             pltpu.VMEM((2, 3, part, width // 2), bf16),
             pltpu.VMEM((16, part), f32),
             pltpu.VMEM((16, part), f32),
             pltpu.VMEM((rows, features // groups), f32),
             pltpu.VMEM((3, rows, features // groups), bf16),
-            pltpu.VMEM((groups, rows, features // groups), bf16),
-            pltpu.VMEM((rows, features // groups), bf16),
-            dma((5,)),
+            pltpu.VMEM((groups + 1, rows, features // groups), bf16),
+            dma((7,)),
             dma((11,)),
             dma((11,)),
-            dma,
-            dma,
+            dma((4,)),
+            dma((4,)),
             dma((2,)),
             dma((2,)),
             dma((2,)),
             dma((2,)),
-            dma((4,)),
-            dma((2,)),
+            dma((3,)),
+            dma,
+            dma,
             dma((2, 4)),
             dma((2, 4)),
             dma((2, 4)),
@@ -662,12 +767,12 @@
             dma((2, 4)),
             dma((2, 4)),
             dma((2, 4)),
-            dma((3,)),
-            dma((groups,)),
-            dma,
+            dma((3, 2)),
+            dma((groups + 1, 2)),
+            dma((9,)),
         ],
         compiler_params=pltpu.CompilerParams(
-            vmem_limit_bytes=52 * 1024 * 1024, collective_id=1, has_side_effects=True
+            vmem_limit_bytes=60 * 1024 * 1024, collective_id=1, has_side_effects=True
         ),
         name="layer",
     )(tokens, *weights, d_out, w_beta.T, b_beta.reshape(1, heads))

time: 61.9 us -> 52.6 us (0.85)
  local copies, waits for them, and re-layouts: 5.2 us -> 0 us
  Pallas kernels: 55.6 us -> 51.7 us
    unnamed x14 -> x0, local copies, waits for them, and re-layouts: 5.2 us -> none
    pallas_call x1, Pallas kernels: 52.4 us -> 48.7 us  [whole_layer(): pl.pallas_call(functools.partial(layer_kernel, groups, heads, dim), out_s...]
where the time goes in v2:
time: 52.6 us; the launch traced here: 52.5 us
  Pallas kernels  51.7 us (98%)
  between operations  0.8 us (2%)
    pallas_call x1, Pallas kernels, whole_layer(): pl.pallas_call(functools.partial(layer_kernel, groups, heads, dim), out_s...  48.7 us
    pallas_call x1, Pallas kernels, place(): pl.pallas_call(functools.partial(place_kernel, count, heads), out_shape=t...  2.94 us

profile of v2, /device:TPU:0, one launch (start us, length us, event | category | flops | bytes accessed | tf_op | source)
XLA Modules:
  0.0 52.5 jit_solution(3097358905465955788)
XLA Ops:
  0.6 48.7 %layer.1 = (bf16[256,512]{1,0:T(8,128)(2,1)}, f32[256,512]{1,0:T(8,128)}, f32[256,512]{1,0:T(8,128)}, f32[256,512]{1,0:T(8,128)}, f32[16,256]{1,0:T(8,128)}) custom-call(bf16[256,2048]{1,0:T(8,128)(2,1)} %x_hbm.1, bf16[2048,512]{1,0:T(8,128)(2,1)} %wq_hbm.1, bf16[2048,512]{1,0:T(8,128)(2,1)} %wk_hbm.1, bf16[2048,512]{1,0:T(8,128)(2,1)} %wv_hbm.1, ...), custom_call_target="tpu_custom_call" | custom-call | tf_op jit(solution)/shard_map/layer/pallas_call | solution.py:708
  49.4 2.9 %place.1 = (bf16[256,512]{1,0:T(8,128)(2,1)}, f32[256,512]{1,0:T(8,128)}, f32[256,512]{1,0:T(8,128)}, f32[256,512]{1,0:T(8,128)}, f32[4,256]{1,0:T(4,128)}, /*index=5*/f32[1,4]{1,0:T(1,128)}) custom-call(bf16[256,512]{1,0:T(8,128)(2,1)} %get-tuple-element.17.refs_0_, f32[256,512]{1,0:T(8,128)} %get-tuple-element.18.refs_1_, ...), custom_call_target="tpu_custom_call" | custom-call | tf_op jit(solution)/shard_map/place/pallas_call | solution.py:680

commit v3 on v2

--- a/solution.py
+++ b/solution.py
@@ -35,6 +35,32 @@
     return total
 
 
+def square_mm(a, b):
+    size = a[0].shape[0]
+    left = jnp.concatenate(a, 1)
+    right = jnp.concatenate(
+        [jnp.concatenate(b, 1), jnp.concatenate([b[0], jnp.zeros_like(b[0])], 1)], 0
+    )
+    both = lax.dot_general(left, right, (((1,), (0,)), ((), ())), preferred_element_type=jnp.float32)
+    return both[:, :size] + both[:, size:]
+
+
+def tight_mm(a, b, dims=(1, 0)):
+    inner, outer = dims[1], 1 - dims[1]
+    size = b[0].shape[outer]
+    left = a[0] if a[1] is None else jnp.concatenate(a, dims[0])
+    right = b[0] if b[1] is None else jnp.concatenate(b, outer)
+    if a[1] is not None:
+        again = b[0]
+        if b[1] is not None:
+            again = jnp.concatenate([b[0], jnp.zeros_like(b[0])], outer)
+        right = jnp.concatenate([right, again], inner)
+    both = lax.dot_general(
+        left, right, (((dims[0],), (dims[1],)), ((), ())), preferred_element_type=jnp.float32
+    )
+    return both if b[1] is None else both[:, :size] + both[:, size:]
+
+
 def iotas(rows, cols):
     return (
         lax.broadcasted_iota(jnp.int32, (rows, cols), 0),
@@ -42,7 +68,8 @@
     )
 
 
-def invert_unit_lower(systems):
+def invert_unit_lower(systems, fillers=()):
+    fillers = list(fillers)
     size = systems[0].shape[0]
     base = min(size, LANES)
     row, col = iotas(base, base)
@@ -56,14 +83,19 @@
         n[i * base : (i + 1) * base, i * base : (i + 1) * base] for n in systems for i in range(count)
     ]
     inverses = [eye - jnp.where(step_mask(1), n, 0.0) for n in diagonals]
+    pairs = [split(n) for n in diagonals]
     s = 2
     while s < base:
-        mask = step_mask(s)
+        mask = jnp.where(step_mask(s), 1.0, 0.0).astype(jnp.bfloat16)
         parts = [split(x) for x in inverses]
-        inner = [mm(split(jnp.where(mask, n, 0.0)), x) for n, x in zip(diagonals, parts)]
-        outer = [mm(x, split(y)) for x, y in zip(parts, inner)]
+        inner = [square_mm((mask * n[0], mask * n[1]), x) for n, x in zip(pairs, parts)]
+        if fillers:
+            fillers.pop(0)()
+        outer = [square_mm(x, split(y)) for x, y in zip(parts, inner)]
         inverses = [x - y for x, y in zip(inverses, outer)]
         s *= 2
+    for filler in fillers:
+        filler()
     grouped = [inverses[i * count : (i + 1) * count] for i in range(len(systems))]
     width = base
     while width < size:
@@ -73,7 +105,7 @@
             for i in range(0, len(blocks), 2):
                 first, second = blocks[i], blocks[i + 1]
                 low = n[(i + 1) * width : (i + 2) * width, i * width : (i + 1) * width]
-                corner = mm(split(second), split(mm(split(low), split(first))))
+                corner = square_mm(split(second), split(square_mm(split(low), split(first))))
                 joined.append(
                     jnp.concatenate(
                         [
@@ -100,21 +132,25 @@
     )
 
 
-def summarise(heads, dim, q_ref, k_ref, v_ref, z_ref, g_ref, put_map):
+def summarise(heads, dim, q_ref, k_ref, v_ref, z_ref, g_ref, put_map, fillers=(), put_unit=None):
     count = q_ref.shape[0]
     row, col = iotas(count, count)
     strict, inclusive = row > col, row >= col
     every = range(heads)
     cols = [slice(h * dim, (h + 1) * dim) for h in every]
-    beta_all = 2.0 * jax.nn.sigmoid(z_ref[...])
+    beta_all = 2.0 * jax.nn.sigmoid(z_ref[:, :heads])
     beta = [beta_all[:, h : h + 1] for h in every]
-    qn = [normalise(q_ref[:, c])[0] for c in cols]
-    kn = [normalise(k_ref[:, c])[0] for c in cols]
+    kp = [normalise(k_ref[:, c]) for c in cols]
+    kn = [x[0] for x in kp]
     ks = [split(x) for x in kn]
-    qs = [split(x) for x in qn]
     gs = [(g_ref[:, c], None) for c in cols]
     gram = [jnp.where(strict, mm(x, x, (1, 1)), 0.0) for x in ks]
-    inverse = [split(t) for t in invert_unit_lower([b * n for b, n in zip(beta, gram)])]
+    systems = [b * n for b, n in zip(beta, gram)]
+    inverse = [split(t) for t in invert_unit_lower(systems, fillers)]
+    qp = [normalise(q_ref[:, c]) for c in cols]
+    qs = [split(x[0]) for x in qp]
+    if put_unit is not None:
+        put_unit(qp, kp)
     gram = [split(n) for n in gram]
     scores = [split(jnp.where(inclusive, mm(a, b, (1, 1)), 0.0)) for a, b in zip(qs, ks)]
     back = [mm(p, g, (0, 0)) for p, g in zip(scores, gs)]
@@ -146,63 +182,42 @@
     summarise(heads, dim, q_ref, k_ref, v_ref, z_ref, g_ref, put_map)(mid_ref)
 
 
-def value_gradients(heads, dim, q_ref, k_ref, z_ref, g_ref, mid_ref, state):
+def gradients(heads, dim, qp, kp, z_ref, g_ref, mid_ref, state, put, strength, valued, between):
     every = range(heads)
-    beta_all = 2.0 * jax.nn.sigmoid(z_ref[...])
-    cols = [slice(h * dim, (h + 1) * dim) for h in every]
+    count = z_ref.shape[0] // 2
+    halves = (slice(0, count), slice(count, 2 * count))
+    row, col = iotas(count, count)
+    strict, inclusive = row > col, row >= col
+    beta_all = 2.0 * jax.nn.sigmoid(z_ref[:, :heads])
     beta = [beta_all[:, h : h + 1] for h in every]
+    ss = [(state(h), None) for h in every]
     ds = [(state(heads + h), None) for h in every]
-    ss = [(state(h), None) for h in every]
     dx = [
         mid_ref[h, :, 2 * dim : 3 * dim] + mm(split(mid_ref[h, :, 3 * dim :]), d, (1, 1))
         for h, d in zip(every, ds)
     ]
     dv = [b * x for b, x in zip(beta, dx)]
-    plain = [
-        mid_ref[h, :, :dim] - mm(split(mid_ref[h, :, dim : 2 * dim]), s, (1, 1))
-        for h, s in zip(every, ss)
-    ]
-    us = [split(b * x) for b, x in zip(beta, plain)]
-    dz = [
-        jnp.sum(x * p, -1, keepdims=True) * b * (1.0 - 0.5 * b) for x, p, b in zip(dx, plain, beta)
-    ]
-    return dv, us, dz
-
-
-def key_gradients(heads, dim, q_ref, k_ref, g_ref, state, dv, us, put, between):
-    every = range(heads)
-    count = q_ref.shape[0] // 2
-    row, col = iotas(count, count)
-    strict, inclusive = row > col, row >= col
-    cols = [slice(h * dim, (h + 1) * dim) for h in every]
-    qp = [normalise(q_ref[:, c]) for c in cols]
-    kp = [normalise(k_ref[:, c]) for c in cols]
-    ks = [split(x[0]) for x in kp]
-    qs = [split(x[0]) for x in qp]
-    gs = [(g_ref[:, c], None) for c in cols]
-    ss = [(state(h), None) for h in every]
-    ds = [(state(heads + h), None) for h in every]
-    dvs = [split(x) for x in dv]
-
-    def top(x):
-        return tuple(None if y is None else y[:count] for y in x)
-
-    def low(x):
-        return tuple(None if y is None else y[count:] for y in x)
-
-    def masked(mask, x):
-        return jnp.concatenate([x[:, :count], jnp.where(mask, x[:, count:], 0.0)], 1)
-
-    inner_top = [split(jnp.where(inclusive, mm(top(g), top(u), (1, 1)), 0.0)) for g, u in zip(gs, us)]
-    pair_top = [jnp.where(strict, mm(top(d), top(u), (1, 1)), 0.0) for d, u in zip(dvs, us)]
-    inner_low = [split(masked(inclusive, mm(low(g), u, (1, 1)))) for g, u in zip(gs, us)]
-    pair_low = [masked(strict, mm(low(d), u, (1, 1))) for d, u in zip(dvs, us)]
-    both_top = [
-        split(jnp.concatenate([e + e.T, f[:, :count].T], 1)) for e, f in zip(pair_top, pair_low)
-    ]
-    both_low = [
-        split(jnp.concatenate([f[:, :count], f[:, count:] + f[:, count:].T], 1)) for f in pair_low
-    ]
+    for h in every:
+        put(2, h, slice(0, 2 * count), dv[h].astype(jnp.bfloat16))
+    valued()
+
+    def pick(x, rows):
+        return tuple(None if y is None else y[rows] for y in x)
+
+    def part(rows):
+        ks = [split(x[0][rows]) for x in kp]
+        qs = [split(x[0][rows]) for x in qp]
+        gs = [(g_ref[rows, h * dim : (h + 1) * dim], None) for h in every]
+        plain = [
+            mid_ref[h, rows, :dim] - mm(split(mid_ref[h, rows, dim : 2 * dim]), s, (1, 1))
+            for h, s in zip(every, ss)
+        ]
+        us = [split(b[rows] * x) for b, x in zip(beta, plain)]
+        dz = [
+            jnp.sum(x[rows] * p, -1, keepdims=True) * b[rows] * (1.0 - 0.5 * b[rows])
+            for x, p, b in zip(dx, plain, beta)
+        ]
+        return ks, qs, gs, us, dz
 
     def through(grad, pair, rows):
         unit, scale = pair[0][rows], pair[1][rows]
@@ -213,25 +228,45 @@
             put(0, h, rows, through(dqn[h], qp[h], rows).astype(jnp.bfloat16))
             put(1, h, rows, through(dkn[h], kp[h], rows).astype(jnp.bfloat16))
 
-    def left(x):
-        return tuple(y[:, :count] for y in x)
-
-    def right(x):
-        return tuple(y[:, count:] for y in x)
-
-    dqn = [mm(top(g), s) + mm(i, top(k)) for g, s, i, k in zip(gs, ss, inner_top, ks)]
+    def below(a, b, mask):
+        found = [tight_mm(x, y, (1, 1)) for x, y in zip(a, b)]
+        return found if mask is None else [jnp.where(mask, x, 0.0) for x in found]
+
+    dvs = [[split(x[rows]) for x in dv] for rows in halves]
+    k0, q0, g0, u0, dz = part(halves[0])
+    strength(halves[0], dz)
+    k1 = [split(x[0][halves[1]]) for x in kp]
+    q1 = [split(x[0][halves[1]]) for x in qp]
+    g1 = [(g_ref[halves[1], h * dim : (h + 1) * dim], None) for h in every]
+    inner0 = [split(x) for x in below(g0, u0, inclusive)]
+    pair0 = below(dvs[0], u0, strict)
+    inner1 = [split(x) for x in below(g1, u0, None)]
+    pair1 = below(dvs[1], u0, None)
+    dqn = [tight_mm(g, s) + tight_mm(i, k) for g, s, i, k in zip(g0, ss, inner0, k0)]
     dkn = [
-        mm(i, top(q), (0, 0)) + mm(left(j), low(q), (0, 0)) + mm(top(u), d) - mm(top(x), s) - mm(e, k)
-        for i, j, q, u, d, x, s, e, k in zip(inner_top, inner_low, qs, us, ds, dvs, ss, both_top, ks)
-    ]
-    finish(slice(0, count), dqn, dkn)
+        tight_mm(i, q, (0, 0)) + tight_mm(j, r, (0, 0)) + tight_mm(u, d) - tight_mm(x, s)
+        - tight_mm(split(e + e.T), k) - tight_mm(split(f.T), l)
+        for i, q, j, r, u, d, x, s, e, k, f, l in zip(
+            inner0, q0, inner1, q1, u0, ds, dvs[0], ss, pair0, k0, pair1, k1
+        )
+    ]
+    finish(halves[0], dqn, dkn)
     between()
-    dqn = [mm(low(g), s) + mm(j, k) for g, s, j, k in zip(gs, ss, inner_low, ks)]
+    k1, q1, g1, u1, dz = part(halves[1])
+    strength(halves[1], dz)
+    inner2 = [split(x) for x in below(g1, u1, inclusive)]
+    pair2 = below(dvs[1], u1, strict)
+    dqn = [
+        tight_mm(g, s) + tight_mm(j, k) + tight_mm(i, l)
+        for g, s, j, k, i, l in zip(g1, ss, inner1, k0, inner2, k1)
+    ]
     dkn = [
-        mm(right(j), low(q), (0, 0)) + mm(low(u), d) - mm(low(x), s) - mm(e, k)
-        for j, q, u, d, x, s, e, k in zip(inner_low, qs, us, ds, dvs, ss, both_low, ks)
-    ]
-    finish(slice(count, 2 * count), dqn, dkn)
+        tight_mm(i, q, (0, 0)) + tight_mm(u, d) - tight_mm(x, s) - tight_mm(split(f), k) - tight_mm(split(e + e.T), l)
+        for i, q, u, d, x, s, f, k, e, l in zip(
+            inner2, q1, u1, ds, dvs[1], ss, pair1, k0, pair2, k1
+        )
+    ]
+    finish(halves[1], dqn, dkn)
 
 
 def strength_lanes(heads, dz):
@@ -253,11 +288,16 @@
     def state(unit):
         return state_ref[unit]
 
-    dv, us, dz = value_gradients(heads, dim, q_ref, k_ref, z_ref, g_ref, mid_ref, state)
-    for h in range(heads):
-        put(2, h, slice(None), dv[h].astype(jnp.bfloat16))
-    key_gradients(heads, dim, q_ref, k_ref, g_ref, state, dv, us, put, lambda: None)
-    out_ref[:, 3 * width :] = strength_lanes(heads, dz).astype(jnp.bfloat16)
+    def strength(rows, dz):
+        out_ref[rows, 3 * width :] = strength_lanes(heads, dz).astype(jnp.bfloat16)
+
+    cols = [slice(h * dim, (h + 1) * dim) for h in range(heads)]
+    qp = [normalise(q_ref[:, c]) for c in cols]
+    kp = [normalise(k_ref[:, c]) for c in cols]
+    gradients(
+        heads, dim, qp, kp, z_ref, g_ref, mid_ref, state, put, strength,
+        lambda: None, lambda: None,
+    )
 
 
 def gathered_states(maps, heads):
@@ -282,7 +322,7 @@
     groups, heads, dim,
     x_hbm, wq_hbm, wk_hbm, wv_hbm, g_hbm, wb_hbm, b_hbm,
     dx_hbm, gq_hbm, gk_hbm, gv_hbm, tail_hbm,
-    dx_ref, grads, tail_ref, x, w, wb, g, wb_ref, b_ref, qkv, z, mid, maps, x_out, x_in, y_out, y_in, state,
+    dx_ref, grads, tail_ref, x, w, wb, g, wb_ref, b_ref, qkv, units, scales, z, mid, maps, x_out, x_in, y_out, y_in, state,
     cols, cols_t, mine, blocks, tails, part_out, part_in, tail_out, tail_in,
     own, piece, landed,
     load, tok_send, tok_recv, map_send, map_recv, x_send, x_recv, f_send, f_recv,
@@ -335,20 +375,19 @@
     def columns(index):
         return pl.ds(pl.multiple_of(index * part, part), part)
 
-    tokens = []
-    for a in range(2):
-        for s in range(1, 4):
-            for b in range(2):
+    tokens, later = {}, [(0, 3, 1), (1, 3, 1)]
+    for s in (2, 3, 1):
+        for b in range(2):
+            for a in range(2):
                 if (a, s, b) != (1, 1, 0):
                     owner = seq(slots[a][s] ^ (partners[a] if b else 0))
                     i = len(tokens)
-                    tokens.append(
-                        remote(
-                            x_hbm.at[:, columns(owner)], cols.at[a, s, b],
-                            tok_send.at[i], tok_recv.at[i], slots[a][s],
-                        )
+                    tokens[a, s, b] = remote(
+                        x_hbm.at[:, columns(owner)], cols.at[a, s, b],
+                        tok_send.at[i], tok_recv.at[i], slots[a][s],
                     )
-                    tokens[i].start()
+                    if (a, s, b) not in later:
+                        tokens[a, s, b].start()
 
     loads[0].wait()
     loads[1].wait()
@@ -356,16 +395,28 @@
     for copy in loads[2:]:
         copy.wait()
     wb[pl.ds(0, heads), :] = wb_ref[...]
-    z[...] = dot(x[...], wb[...], (1, 1))
-    z[:, :heads] = z[:, :heads] + b_ref[...]
-    qkv[0] = dot(x[...], w[0])
-    qkv[2] = dot(x[...], w[2])
-
+    z[:, :heads] = dot(x[...], wb[:16], (1, 1))[:, :heads] + b_ref[...]
     def put_map(unit, factor, offset):
         maps[core, unit, 0] = factor.astype(bf16)
         maps[core, unit, 1] = offset.astype(bf16)
 
-    put_mid = summarise(heads, dim, qkv.at[0], qkv.at[1], qkv.at[2], z, g, put_map)
+    def project(i, n):
+        def run():
+            span = slice(n * width // 2, (n + 1) * width // 2)
+            qkv[i, :, span] = dot(x[...], w[i, :, span])
+
+        return run
+
+    def put_unit(qp, kp):
+        for i, pairs in enumerate((qp, kp)):
+            for h, (unit, scale) in enumerate(pairs):
+                units[i, :, h * dim : (h + 1) * dim] = unit
+                scales[:, i * heads + h : i * heads + h + 1] = scale
+
+    fillers = [project(i, n) for i in (0, 2) for n in range(2)]
+    put_mid = summarise(
+        heads, dim, qkv.at[0], qkv.at[1], qkv.at[2], z, g, put_map, fillers, put_unit
+    )
     passed, taken = across, 1 - across
     kept, other = pl.ds(core * half, half), pl.ds((1 - core) * half, half)
     urgent = [
@@ -418,17 +469,22 @@
     def own_columns(a, b):
         return x[:, columns(seq(partners[a]) if b else me)]
 
+    def turn_block(a, s, b):
+        if s == 0:
+            block = own_columns(a, b)
+        else:
+            block = cols[0, 1, 0] if (a, s, b) == (1, 1, 0) else cols[a, s, b]
+        cols_t[a, b * part : (b + 1) * part, s * rows : (s + 1) * rows] = block.T
+
     def turn(a):
         for s in range(4):
             for b in range(2):
-                if s == 0:
-                    block = own_columns(a, b)
-                else:
-                    block = cols[0, 1, 0] if (a, s, b) == (1, 1, 0) else cols[a, s, b]
-                cols_t[a, b * part : (b + 1) * part, s * rows : (s + 1) * rows] = block.T
-
-    for copy in tokens:
-        copy.wait_recv()
+                if (a, s, b) not in later:
+                    turn_block(a, s, b)
+
+    for key, copy in tokens.items():
+        if key[0] == 0 and key not in later:
+            copy.wait_recv()
     turn(0)
     over[0].wait_recv()
     for n, (factor, offset) in enumerate(totals):
@@ -445,6 +501,11 @@
     forward[0].start()
     over[1].wait_recv()
     forward[1].start()
+    for key in later:
+        tokens[key].start()
+    for key, copy in tokens.items():
+        if key[0] == 1 and key not in later:
+            copy.wait_recv()
     turn(1)
     for copy in forward + arriving[2:]:
         copy.wait_recv()
@@ -494,15 +555,21 @@
         for copy in spreads[key][:2]:
             copy.start()
 
-    dv, us, dz = value_gradients(heads, dim, qkv.at[0], qkv.at[1], z, g, mid, unit_state)
-    for h in range(heads):
-        put(2, h, slice(0, rows), dv[h].astype(bf16))
-    send((0, 2))
-    send((1, 2))
-    last = strength_lanes(heads, dz)
-    mine[:, 3 * width :] = last.astype(bf16)
-    tails[0] = last.T[:16].astype(bf16)
-    send((0, 3))
+    def valued():
+        send((0, 2))
+        send((1, 2))
+
+    def strength(span, dz):
+        last = strength_lanes(heads, dz)
+        mine[span, 3 * width :] = last.astype(bf16)
+        tails[0, :, span] = last.T[:16].astype(bf16)
+
+    def unit_pairs(i):
+        return [
+            (units[i, :, h * dim : (h + 1) * dim], scales[:, i * heads + h : i * heads + h + 1])
+            for h in range(heads)
+        ]
+
     halves = [slice(0, rows // 2), slice(rows // 2, rows)]
 
     def input_part(index, rows):
@@ -533,10 +600,11 @@
         piece[0, halves[h]] = input_part(targets[0], halves[h]).astype(bf16)
         landing(0, h).start()
 
-    key_gradients(
-        heads, dim, qkv.at[0], qkv.at[1], g, unit_state, dv, us, put, lambda: first_piece(0)
-    )
-    for key in ((0, 0), (1, 0), (0, 1), (1, 1)):
+    gradients(
+        heads, dim, unit_pairs(0), unit_pairs(1), z, g, mid, unit_state, put, strength,
+        valued, lambda: first_piece(0),
+    )
+    for key in ((0, 0), (1, 0), (0, 1), (1, 1), (0, 3)):
         send(key)
     first_piece(1)
     piece[1] = input_part(targets[1], slice(0, rows)).astype(bf16)
@@ -564,7 +632,7 @@
             piece[2, halves[h]] = (piece[2, halves[h]].astype(f32) + arrived(groups, h)).astype(bf16)
             landing(2, h).start()
 
-    order = [(0, 2), (1, 2), (0, 3), (0, 0), (1, 0), (0, 1), (1, 1)]
+    order = [(0, 2), (1, 2), (0, 0), (1, 0), (0, 1), (1, 1), (0, 3)]
     trades = {
         (a, i): remote(
             part_out.at[a, i], part_in.at[a, i], part_send.at[a, i], part_recv.at[a, i], partners[a]
@@ -595,14 +663,17 @@
             tail_trade.start()
             tail_ref[...] = jnp.where(row == 8, held, sums[0])
 
+    for key in later:
+        tokens[key].wait_recv()
+        turn_block(*key)
     for n, key in enumerate(order):
         spreads[key][0].wait_recv()
         spreads[key][2].start()
         if n > 0:
             process(*order[n - 1])
-        if n == 2:
+        if n == 1:
             pass_on(0)
-        if n == 4:
+        if n == 3:
             pass_on(1)
 
     process(*order[-1])
@@ -645,7 +716,7 @@
     for n in range(3):
         for h in range(2):
             landing(n, h).wait_send()
-    for copy in sibling + tokens + over + forward + [tail_trade] + list(trades.values()):
+    for copy in sibling + list(tokens.values()) + over + forward + [tail_trade] + list(trades.values()):
         copy.wait_send()
     for copies in spreads.values():
         for copy in copies:
@@ -657,16 +728,24 @@
 def place_kernel(count, heads, *refs):
     sources, outs = refs[: count + 1], refs[count + 1 : 2 * count + 3]
     held, sems = refs[2 * count + 3 : -1], refs[-1]
-    fetch = [
-        pltpu.make_async_copy(sources[i], held[i], sems.at[0, i]) for i in range(count + 1)
-    ]
-    store = [pltpu.make_async_copy(held[i], outs[i], sems.at[1, i]) for i in range(count)]
+    fetch, store = [], []
+    for i in range(count):
+        size = sources[i].shape[0] // 2
+        for n in range(2):
+            span = pl.ds(n * size, size)
+            j = 2 * i + n
+            fetch.append(
+                pltpu.make_async_copy(sources[i].at[span], held[i].at[span], sems.at[0, j])
+            )
+            store.append(pltpu.make_async_copy(held[i].at[span], outs[i].at[span], sems.at[1, j]))
+    small = pltpu.make_async_copy(sources[count], held[count], sems.at[0, 2 * count])
     for copy in fetch:
         copy.start()
-    for i in range(count):
-        fetch[i].wait()
-        store[i].start()
-    fetch[count].wait()
+    small.start()
+    for j in range(2 * count):
+        fetch[j].wait()
+        store[j].start()
+    small.wait()
     outs[count][...] = held[count][:heads, :]
     outs[count + 1][...] = held[count][8:9, :heads] + held[count][8:9, heads : 2 * heads]
     for copy in store:
@@ -687,7 +766,7 @@
         in_specs=[hbm] * (count + 1),
         out_specs=(hbm,) * count + (vmem,) * 2,
         scratch_shapes=[pltpu.VMEM(a.shape, a.dtype) for a in (*arrays, tail)]
-        + [pltpu.SemaphoreType.DMA((2, count + 1))],
+        + [pltpu.SemaphoreType.DMA((2, 2 * count + 1))],
         compiler_params=pltpu.CompilerParams(vmem_limit_bytes=60 * 1024 * 1024),
         name="place",
     )(*arrays, tail)
@@ -727,6 +806,8 @@
             pltpu.VMEM((heads, features), bf16),
             pltpu.VMEM((1, heads), f32),
             pltpu.VMEM((3, rows, width), f32),
+            pltpu.VMEM((2, rows, width), f32),
+            pltpu.VMEM((rows, LANES), f32),
             pltpu.VMEM((rows, LANES), f32),
             pltpu.VMEM((heads, rows, 4 * dim), f32),
             pltpu.VMEM((2, 2 * heads, 2, dim, dim), bf16),

time: 52.6 us -> 51.3 us (0.975)
  Pallas kernels: 51.7 us -> 50.4 us
    pallas_call x1, Pallas kernels: 48.7 us -> 47.4 us  [whole_layer(): pl.pallas_call(functools.partial(layer_kernel, groups, heads, dim), out_s...]
where the time goes in v3:
time: 51.3 us; the launch traced here: 51.2 us
  Pallas kernels  50.4 us (98%)
  between operations  0.8 us (2%)
    pallas_call x1, Pallas kernels, whole_layer(): pl.pallas_call(functools.partial(layer_kernel, groups, heads, dim), out_s...  47.4 us
    pallas_call x1, Pallas kernels, place(): pl.pallas_call(functools.partial(place_kernel, count, heads), out_shape=t...  2.97 us

profile of v3, /device:TPU:0, one launch (start us, length us, event | category | flops | bytes accessed | tf_op | source)
XLA Modules:
  0.0 51.2 jit_solution(2831599428823880892)
XLA Ops:
  0.6 47.4 %layer.1 = (bf16[256,512]{1,0:T(8,128)(2,1)}, f32[256,512]{1,0:T(8,128)}, f32[256,512]{1,0:T(8,128)}, f32[256,512]{1,0:T(8,128)}, f32[16,256]{1,0:T(8,128)}) custom-call(bf16[256,2048]{1,0:T(8,128)(2,1)} %x_hbm.1, bf16[2048,512]{1,0:T(8,128)(2,1)} %wq_hbm.1, bf16[2048,512]{1,0:T(8,128)(2,1)} %wk_hbm.1, bf16[2048,512]{1,0:T(8,128)(2,1)} %wv_hbm.1, ...), custom_call_target="tpu_custom_call" | custom-call | tf_op jit(solution)/shard_map/layer/pallas_call | solution.py:787
  48.1 3.0 %place.1 = (bf16[256,512]{1,0:T(8,128)(2,1)}, f32[256,512]{1,0:T(8,128)}, f32[256,512]{1,0:T(8,128)}, f32[256,512]{1,0:T(8,128)}, f32[4,256]{1,0:T(4,128)}, /*index=5*/f32[1,4]{1,0:T(1,128)}) custom-call(bf16[256,512]{1,0:T(8,128)(2,1)} %get-tuple-element.17.refs_0_, f32[256,512]{1,0:T(8,128)} %get-tuple-element.18.refs_1_, ...), custom_call_target="tpu_custom_call" | custom-call | tf_op jit(solution)/shard_map/place/pallas_call | solution.py:759

commit v4 on v3

--- a/solution.py
+++ b/solution.py
@@ -59,6 +59,18 @@
         left, right, (((dims[0],), (dims[1],)), ((), ())), preferred_element_type=jnp.float32
     )
     return both if b[1] is None else both[:, :size] + both[:, size:]
+
+
+def wide_mm(a, b, dims=(1, 0)):
+    numbers = (((dims[0],), (dims[1],)), ((), ()))
+    size = b[0].shape[1 - dims[1]]
+    both = lax.dot_general(
+        a[0], jnp.concatenate(b, 1 - dims[1]), numbers, preferred_element_type=jnp.float32
+    )
+    total = both[:, :size] + both[:, size:]
+    if a[1] is not None:
+        total = total + lax.dot_general(a[1], b[0], numbers, preferred_element_type=jnp.float32)
+    return total
 
 
 def iotas(rows, cols):
@@ -159,9 +171,9 @@
     adjoint = [
         mm(t, split(jnp.concatenate([p, k], 1)), (0, 0)) for t, p, k in zip(inverse, back, kn)
     ]
-    ends = [mm(f, k, (0, 0)) for f, k in zip(forth, ks)]
-    tails = [mm(split(a), split(b * k), (0, 0)) for a, b, k in zip(adjoint, beta, kn)]
-    direct = [mm(g, q, (0, 0)) for g, q in zip(gs, qs)]
+    ends = [wide_mm(f, k, (0, 0)) for f, k in zip(forth, ks)]
+    tails = [wide_mm(split(a), split(b * k), (0, 0)) for a, b, k in zip(adjoint, beta, kn)]
+    direct = [wide_mm(g, q, (0, 0)) for g, q in zip(gs, qs)]
     for h in every:
         put_map(h, ends[h][dim:], ends[h][:dim])
         put_map(heads + h, tails[h][dim:], direct[h] - tails[h][:dim])
@@ -193,7 +205,7 @@
     ss = [(state(h), None) for h in every]
     ds = [(state(heads + h), None) for h in every]
     dx = [
-        mid_ref[h, :, 2 * dim : 3 * dim] + mm(split(mid_ref[h, :, 3 * dim :]), d, (1, 1))
+        mid_ref[h, :, 2 * dim : 3 * dim] + tight_mm(split(mid_ref[h, :, 3 * dim :]), d, (1, 1))
         for h, d in zip(every, ds)
     ]
     dv = [b * x for b, x in zip(beta, dx)]
@@ -209,7 +221,7 @@
         qs = [split(x[0][rows]) for x in qp]
         gs = [(g_ref[rows, h * dim : (h + 1) * dim], None) for h in every]
         plain = [
-            mid_ref[h, rows, :dim] - mm(split(mid_ref[h, rows, dim : 2 * dim]), s, (1, 1))
+            mid_ref[h, rows, :dim] - tight_mm(split(mid_ref[h, rows, dim : 2 * dim]), s, (1, 1))
             for h, s in zip(every, ss)
         ]
         us = [split(b[rows] * x) for b, x in zip(beta, plain)]
@@ -489,7 +501,7 @@
     over[0].wait_recv()
     for n, (factor, offset) in enumerate(totals):
         entering = x_in[0, core * half + n]
-        y_out[n] = (entering.astype(f32) - mm((entering, None), split(factor)) + offset).astype(bf16)
+        y_out[n] = (entering.astype(f32) - tight_mm((entering, None), split(factor)) + offset).astype(bf16)
     up = [remote(y_out, y_in.at[kept], y_send.at[j], y_recv, 4 + 2 * j) for j in range(2)]
     share = remote(y_in.at[kept], y_in.at[kept], y_send.at[2], s_recv, 1)
 
@@ -518,7 +530,7 @@
         unit = inside * heads + h
         factor = maps[inside, unit, 0]
         before = state[unit]
-        state[unit] = before - mm(split(before), (factor, None)) + maps[inside, unit, 1].astype(f32)
+        state[unit] = before - tight_mm(split(before), (factor, None)) + maps[inside, unit, 1].astype(f32)
         first = jnp.where(taken == lead, x_in[1, h].astype(f32), 0.0).astype(bf16)
         second = jnp.where(inside == lead, factor.astype(f32), 0.0).astype(bf16)
         bridge.append(split(first.astype(f32) + second.astype(f32) - dot(first, second)))
@@ -527,7 +539,7 @@
     share.wait_recv()
     for h in range(heads):
         unit = lead * heads + h
-        state[unit] = state[unit] + (y_in[h].astype(f32) - mm((y_in[h], None), bridge[h]))
+        state[unit] = state[unit] + (y_in[h].astype(f32) - tight_mm((y_in[h], None), bridge[h]))
 
     def put(i, h, span, value):
         a, n = h // half, h % half
@@ -727,7 +739,7 @@
 
 def place_kernel(count, heads, *refs):
     sources, outs = refs[: count + 1], refs[count + 1 : 2 * count + 3]
-    held, sems = refs[2 * count + 3 : -1], refs[-1]
+    held, (strength, bias, sems) = refs[2 * count + 3 : -3], refs[-3:]
     fetch, store = [], []
     for i in range(count):
         size = sources[i].shape[0] // 2
@@ -739,22 +751,25 @@
             )
             store.append(pltpu.make_async_copy(held[i].at[span], outs[i].at[span], sems.at[1, j]))
     small = pltpu.make_async_copy(sources[count], held[count], sems.at[0, 2 * count])
+    small.start()
     for copy in fetch:
         copy.start()
-    small.start()
+    small.wait()
+    strength[...] = held[count][:heads, :]
+    bias[...] = held[count][8:9, :heads] + held[count][8:9, heads : 2 * heads]
+    store.append(pltpu.make_async_copy(strength, outs[count], sems.at[1, 2 * count]))
+    store.append(pltpu.make_async_copy(bias, outs[count + 1], sems.at[1, 2 * count + 1]))
+    for copy in store[-2:]:
+        copy.start()
     for j in range(2 * count):
         fetch[j].wait()
         store[j].start()
-    small.wait()
-    outs[count][...] = held[count][:heads, :]
-    outs[count + 1][...] = held[count][8:9, :heads] + held[count][8:9, heads : 2 * heads]
     for copy in store:
         copy.wait()
 
 
 def place(arrays, tail, heads):
     count = len(arrays)
-    vmem = pl.BlockSpec(memory_space=pltpu.VMEM)
     hbm = pl.BlockSpec(memory_space=pltpu.HBM)
     return pl.pallas_call(
         functools.partial(place_kernel, count, heads),
@@ -764,9 +779,13 @@
             jax.ShapeDtypeStruct((1, heads), tail.dtype),
         ),
         in_specs=[hbm] * (count + 1),
-        out_specs=(hbm,) * count + (vmem,) * 2,
+        out_specs=(hbm,) * (count + 2),
         scratch_shapes=[pltpu.VMEM(a.shape, a.dtype) for a in (*arrays, tail)]
-        + [pltpu.SemaphoreType.DMA((2, 2 * count + 1))],
+        + [
+            pltpu.VMEM((heads, tail.shape[1]), tail.dtype),
+            pltpu.VMEM((1, heads), tail.dtype),
+            pltpu.SemaphoreType.DMA((2, 2 * count + 2)),
+        ],
         compiler_params=pltpu.CompilerParams(vmem_limit_bytes=60 * 1024 * 1024),
         name="place",
     )(*arrays, tail)

time: 51.3 us -> 50.2 us (0.979)
  Pallas kernels: 50.4 us -> 49.1 us
    pallas_call x1, Pallas kernels: 47.4 us -> 46.7 us  [whole_layer(): pl.pallas_call(functools.partial(layer_kernel, groups, heads, dim), out_s...]
    pallas_call x1, Pallas kernels: 2.97 us -> 2.41 us  [place(): pl.pallas_call(functools.partial(place_kernel, count, heads), out_shape=t...]
where the time goes in v4:
time: 50.2 us; the launch traced here: 49.9 us
  Pallas kernels  49.1 us (98%)
  between operations  0.8 us (2%)
    pallas_call x1, Pallas kernels, whole_layer(): pl.pallas_call(functools.partial(layer_kernel, groups, heads, dim), out_s...  46.7 us
    pallas_call x1, Pallas kernels, place(): pl.pallas_call(functools.partial(place_kernel, count, heads), out_shape=t...  2.41 us

profile of v4, /device:TPU:0, one launch (start us, length us, event | category | flops | bytes accessed | tf_op | source)
XLA Modules:
  0.0 49.9 jit_solution(11152801654399255683)
XLA Ops:
  0.6 46.7 %layer.1 = (bf16[256,512]{1,0:T(8,128)(2,1)}, f32[256,512]{1,0:T(8,128)}, f32[256,512]{1,0:T(8,128)}, f32[256,512]{1,0:T(8,128)}, f32[16,256]{1,0:T(8,128)}) custom-call(bf16[256,2048]{1,0:T(8,128)(2,1)} %x_hbm.1, bf16[2048,512]{1,0:T(8,128)(2,1)} %wq_hbm.1, bf16[2048,512]{1,0:T(8,128)(2,1)} %wk_hbm.1, bf16[2048,512]{1,0:T(8,128)(2,1)} %wv_hbm.1, ...), custom_call_target="tpu_custom_call" | custom-call | tf_op jit(solution)/shard_map/layer/pallas_call | solution.py:806
  47.4 2.4 %place.1 = (bf16[256,512]{1,0:T(8,128)(2,1)}, f32[256,512]{1,0:T(8,128)}, f32[256,512]{1,0:T(8,128)}, f32[256,512]{1,0:T(8,128)}, f32[4,256]{1,0:T(4,128)}, /*index=5*/f32[1,4]{1,0:T(1,128)}) custom-call(bf16[256,512]{1,0:T(8,128)(2,1)} %get-tuple-element.17.refs_0_, f32[256,512]{1,0:T(8,128)} %get-tuple-element.18.refs_1_, ...), custom_call_target="tpu_custom_call" | custom-call | tf_op jit(solution)/shard_map/place/pallas_call | solution.py:774

commit v5 on v4

--- a/solution.py
+++ b/solution.py
@@ -71,6 +71,14 @@
     if a[1] is not None:
         total = total + lax.dot_general(a[1], b[0], numbers, preferred_element_type=jnp.float32)
     return total
+
+
+def deep_mm(a, b):
+    numbers = (((1,), (1,)), ((), ()))
+    dot = functools.partial(
+        lax.dot_general, dimension_numbers=numbers, preferred_element_type=jnp.float32
+    )
+    return dot(jnp.concatenate(a, 1), jnp.concatenate([b[0], b[0]], 1)) + dot(a[0], b[1])
 
 
 def iotas(rows, cols):
@@ -156,16 +164,27 @@
     kn = [x[0] for x in kp]
     ks = [split(x) for x in kn]
     gs = [(g_ref[:, c], None) for c in cols]
-    gram = [jnp.where(strict, mm(x, x, (1, 1)), 0.0) for x in ks]
+    gram = [jnp.where(strict, deep_mm(x, x), 0.0) for x in ks]
     systems = [b * n for b, n in zip(beta, gram)]
+    late = {}
+
+    def score():
+        qp = [normalise(q_ref[:, c]) for c in cols]
+        late["qs"] = [split(x[0]) for x in qp]
+        if put_unit is not None:
+            put_unit(qp, kp)
+        late["scores"] = [
+            split(jnp.where(inclusive, deep_mm(a, b), 0.0)) for a, b in zip(late["qs"], ks)
+        ]
+
+    def pull():
+        late["back"] = [mm(p, g, (0, 0)) for p, g in zip(late["scores"], gs)]
+        late["direct"] = [wide_mm(g, q, (0, 0)) for g, q in zip(gs, late["qs"])]
+
+    fillers = list(fillers) + [score, pull]
     inverse = [split(t) for t in invert_unit_lower(systems, fillers)]
-    qp = [normalise(q_ref[:, c]) for c in cols]
-    qs = [split(x[0]) for x in qp]
-    if put_unit is not None:
-        put_unit(qp, kp)
     gram = [split(n) for n in gram]
-    scores = [split(jnp.where(inclusive, mm(a, b, (1, 1)), 0.0)) for a, b in zip(qs, ks)]
-    back = [mm(p, g, (0, 0)) for p, g in zip(scores, gs)]
+    back, direct = late["back"], late["direct"]
     forth_in = [jnp.concatenate([v_ref[:, c], k], 1) for c, k in zip(cols, kn)]
     forth = [split(mm(t, split(b * x))) for t, b, x in zip(inverse, beta, forth_in)]
     adjoint = [
@@ -173,7 +192,6 @@
     ]
     ends = [wide_mm(f, k, (0, 0)) for f, k in zip(forth, ks)]
     tails = [wide_mm(split(a), split(b * k), (0, 0)) for a, b, k in zip(adjoint, beta, kn)]
-    direct = [wide_mm(g, q, (0, 0)) for g, q in zip(gs, qs)]
     for h in every:
         put_map(h, ends[h][dim:], ends[h][:dim])
         put_map(heads + h, tails[h][dim:], direct[h] - tails[h][:dim])
@@ -629,8 +647,6 @@
         for h in range(2):
             landing(2, h).start()
 
-    own[...] = input_part(group, slice(0, rows))
-
     def arrived(slot, h):
         remote(
             piece.at[0, halves[h]], landed.at[slot, halves[h]],
@@ -689,6 +705,7 @@
             pass_on(1)
 
     process(*order[-1])
+    own[...] = input_part(group, slice(0, rows))
     saves = []
 
     def keep(source, target):

time: 50.2 us -> 49.8 us (level)
  no operation moved by 1% of the time
where the time goes in v5:
time: 49.8 us; the launch traced here: 49.5 us
  Pallas kernels  48.7 us (98%)
  between operations  0.8 us (2%)
    pallas_call x1, Pallas kernels, whole_layer(): pl.pallas_call(functools.partial(layer_kernel, groups, heads, dim), out_s...  46.3 us
    pallas_call x1, Pallas kernels, place(): pl.pallas_call(functools.partial(place_kernel, count, heads), out_shape=t...  2.41 us

profile of v5, /device:TPU:0, one launch (start us, length us, event | category | flops | bytes accessed | tf_op | source)
XLA Modules:
  0.0 49.5 jit_solution(10585751365777199784)
XLA Ops:
  0.6 46.3 %layer.1 = (bf16[256,512]{1,0:T(8,128)(2,1)}, f32[256,512]{1,0:T(8,128)}, f32[256,512]{1,0:T(8,128)}, f32[256,512]{1,0:T(8,128)}, f32[16,256]{1,0:T(8,128)}) custom-call(bf16[256,2048]{1,0:T(8,128)(2,1)} %x_hbm.1, bf16[2048,512]{1,0:T(8,128)(2,1)} %wq_hbm.1, bf16[2048,512]{1,0:T(8,128)(2,1)} %wk_hbm.1, bf16[2048,512]{1,0:T(8,128)(2,1)} %wv_hbm.1, ...), custom_call_target="tpu_custom_call" | custom-call | tf_op jit(solution)/shard_map/layer/pallas_call | solution.py:823
  47.0 2.4 %place.1 = (bf16[256,512]{1,0:T(8,128)(2,1)}, f32[256,512]{1,0:T(8,128)}, f32[256,512]{1,0:T(8,128)}, f32[256,512]{1,0:T(8,128)}, f32[4,256]{1,0:T(4,128)}, /*index=5*/f32[1,4]{1,0:T(1,128)}) custom-call(bf16[256,512]{1,0:T(8,128)(2,1)} %get-tuple-element.17.refs_0_, f32[256,512]{1,0:T(8,128)} %get-tuple-element.18.refs_1_, ...), custom_call_target="tpu_custom_call" | custom-call | tf_op jit(solution)/shard_map/place/pallas_call | solution.py:791

commit v6 on v5

--- a/solution.py
+++ b/solution.py
@@ -475,23 +475,18 @@
     put_mid(mid)
     arriving[0].wait_recv()
 
-    def chip_total(way, n):
+    def chip_part(way, n, j):
         unit = way * heads + core * half + n
-        first = jnp.concatenate([maps[way, unit, 0], maps[way, unit, 1]], 0)
-        factor = maps[1 - way, unit, 0]
-        moved = dot(first, factor)
-        both = first.astype(f32) - moved
-        return both[:dim] + factor.astype(f32), both[dim:] + maps[1 - way, unit, 1].astype(f32)
-
-    for n in range(half):
-        factor, offset = chip_total(passed, n)
-        x_out[0, n] = offset.astype(bf16)
-        x_out[1, n] = factor.astype(bf16)
+        first, second = maps[way, unit, j], maps[1 - way, unit, j]
+        return first.astype(f32) - dot(first, maps[1 - way, unit, 0]) + second.astype(f32)
+
     over = [remote(x_out.at[j], x_in.at[j, kept], x_send.at[j], x_recv.at[j], 2) for j in range(2)]
-    for copy in over:
-        copy.start()
+    for j in range(2):
+        for n in range(half):
+            x_out[j, n] = chip_part(passed, n, 1 - j).astype(bf16)
+        over[j].start()
     arriving[1].wait_recv()
-    totals = [chip_total(taken, n) for n in range(half)]
+    totals = [(chip_part(taken, n, 0), chip_part(taken, n, 1)) for n in range(half)]
     forward = [
         remote(x_in.at[j, kept], x_in.at[j, kept], f_send.at[j], f_recv.at[j], 1) for j in range(2)
     ]
@@ -525,7 +520,7 @@
 
     @pl.when(upper == taken)
     def _():
-        for copy in up:
+        for copy in up[::-1]:
             copy.start()
 
     forward[0].start()

time: 49.8 us -> 49.8 us (level)
  no operation moved by 1% of the time
where the time goes in v6:
time: 49.8 us; the launch traced here: 49.5 us
  Pallas kernels  48.7 us (98%)
  between operations  0.8 us (2%)
    pallas_call x1, Pallas kernels, whole_layer(): pl.pallas_call(functools.partial(layer_kernel, groups, heads, dim), out_s...  46.3 us
    pallas_call x1, Pallas kernels, place(): pl.pallas_call(functools.partial(place_kernel, count, heads), out_shape=t...  2.41 us

profile of v6, /device:TPU:0, one launch (start us, length us, event | category | flops | bytes accessed | tf_op | source)
XLA Modules:
  0.0 49.5 jit_solution(3193716413366125088)
XLA Ops:
  0.6 46.3 %layer.1 = (bf16[256,512]{1,0:T(8,128)(2,1)}, f32[256,512]{1,0:T(8,128)}, f32[256,512]{1,0:T(8,128)}, f32[256,512]{1,0:T(8,128)}, f32[16,256]{1,0:T(8,128)}) custom-call(bf16[256,2048]{1,0:T(8,128)(2,1)} %x_hbm.1, bf16[2048,512]{1,0:T(8,128)(2,1)} %wq_hbm.1, bf16[2048,512]{1,0:T(8,128)(2,1)} %wk_hbm.1, bf16[2048,512]{1,0:T(8,128)(2,1)} %wv_hbm.1, ...), custom_call_target="tpu_custom_call" | custom-call | tf_op jit(solution)/shard_map/layer/pallas_call | solution.py:818
  46.9 2.4 %place.1 = (bf16[256,512]{1,0:T(8,128)(2,1)}, f32[256,512]{1,0:T(8,128)}, f32[256,512]{1,0:T(8,128)}, f32[256,512]{1,0:T(8,128)}, f32[4,256]{1,0:T(4,128)}, /*index=5*/f32[1,4]{1,0:T(1,128)}) custom-call(bf16[256,512]{1,0:T(8,128)(2,1)} %get-tuple-element.17.refs_0_, f32[256,512]{1,0:T(8,128)} %get-tuple-element.18.refs_1_, ...), custom_call_target="tpu_custom_call" | custom-call | tf_op jit(solution)/shard_map/place/pallas_call | solution.py:786
